TPU v7x, 256 devices: a whole 4x4x8 slice. The times are simulated.
256 devices in a mesh: expert: 32 (over y, x, core), narrow: 8 (over z).
Axes of the slice: x: 4, y: 4, z: 8, core: 2. Of those that a mesh axis runs over, the one named last changes fastest.
Arguments:
- feats: bfloat16 [262144, 512], P(('expert', 'narrow')), may hold values from -6 to 6
- cotangent: bfloat16 [262144, 512], P(('expert', 'narrow')), may hold values from -0.59765625 to 0.59765625
- routes: int32 [262144, 1], P(('expert', 'narrow')), may hold values from 0 to 31; in each aligned block of 1024 rows (0 to 1023, 1024 to 2047, ...) at most 64 rows name the same one
- image_ids: int32 [262144], P(('expert', 'narrow')), may hold values from 0 to 2047, as said below
- codes: bfloat16 [2048, 48], replicated, may hold values from -6 to 6
- params: bfloat16 [32, 2096, 512], P('expert', 'narrow'), may hold values from -0.375 to 0.375
Outputs:
- out_rows: bfloat16 [262144, 512], P(('expert', 'narrow'))
- feat_grad: bfloat16 [262144, 512], P(('expert', 'narrow'))
- param_grad: float32 [32, 2096, 512], P('expert', 'narrow')
- code_grad: float32 [2048, 48], P(('expert', 'narrow'))
Inputs may be any that keep to these rules, and one draw needn't show every extreme that they name: `routes`: among the rows of one device no expert is named more than 64 times, and on some device some expert is named exactly 64 times. `image_ids`: the rows of the device with flat index f over expert+narrow (expert index slowest) name only images f * 8 to f * 8 + 2 * 8 - 1, taken modulo 2048.
All inputs are finite; a program needn't handle non-finite values.
Results may differ from a plain program's by a relative error of at most 0.017.
Values may be sent and summed in bfloat16 or wider, within the bound.
No kernel may reach another device: no remote copies, remote signals or barrier semaphores. Data moves between devices by JAX's collectives and lax.ppermute only.
A program may use at most 128 MiB of HBM per device.

v0:
```python
import jax
import jax.numpy as jnp
from jax import lax
from jax.experimental import pallas as pl
from jax.experimental.pallas import tpu as pltpu
from jax.sharding import PartitionSpec as P

LAYERS = 4
D = 512
CODE = 48
ROWS_DEV = 1024
IMG_DEV = 8
CAP = 64
PEERS = 32
NARROW = 8
LANES = 128
CHUNKS = D // LANES
TAIL = 8
BLOCK = 2 * CHUNKS * CAP + TAIL
SHARD = 262
SHARD_PAD = 264
PROWS = 2096
F32 = jnp.float32
BF16 = jnp.bfloat16
VMEM = 56 * 1024 * 1024


def params_of(semantics=None):
    return pltpu.CompilerParams(vmem_limit_bytes=VMEM, dimension_semantics=semantics)


def dot(a, b, ca=1, cb=0):
    return lax.dot_general(a, b, (((ca,), (cb,)), ((), ())), preferred_element_type=F32)


PACK_PEERS = 8


def pack_body(first_ref, routes_ref, ids_ref, feats_ref, cot_ref, out_ref, pos_ref, pos_scr, off_scr):
    step = pl.program_id(0)

    @pl.when(step == 0)
    def _():
        width = 256
        upper = (
            lax.broadcasted_iota(jnp.int32, (width, width), 0)
            <= lax.broadcasted_iota(jnp.int32, (width, width), 1)
        ).astype(F32).astype(BF16)
        expert = lax.broadcasted_iota(jnp.int32, (PEERS, width), 0)
        base = (expert * CAP - 1).astype(F32)
        carry = jnp.zeros((PEERS, 1), F32)
        for b in range(ROWS_DEV // width):
            hot = (routes_ref[:, b * width : (b + 1) * width] == expert).astype(F32)
            rank = dot(hot.astype(BF16), upper) + carry
            place = jnp.sum(hot * (rank + base), axis=0, keepdims=True)
            carry = carry + jnp.sum(hot, axis=1, keepdims=True)
            pos_scr[:, b * width : (b + 1) * width] = jnp.broadcast_to(place.astype(jnp.int32), (8, width))
        off = ids_ref[...] - first_ref[0]
        off = jnp.where(off < 0, off + PEERS * NARROW * IMG_DEV, off) + 1
        off_scr[...] = jnp.broadcast_to(off.astype(F32), (16, ROWS_DEV)).astype(BF16)
        pos_ref[...] = pos_scr[...]

    n = PACK_PEERS * CAP
    slot = lax.broadcasted_iota(jnp.int32, (n, ROWS_DEV), 0) + step * n
    pick = (pos_scr[0:1, :] == slot).astype(F32).astype(BF16)
    for half, src in enumerate((feats_ref, cot_ref)):
        got = dot(pick, src[...]).astype(BF16)
        for j in range(PACK_PEERS):
            for c in range(CHUNKS):
                r = (half * CHUNKS + c) * CAP
                out_ref[j, r : r + CAP, :] = got[j * CAP : (j + 1) * CAP, c * LANES : (c + 1) * LANES]
    tail = dot(off_scr[...], pick, 1, 1)[:TAIL]
    for j in range(PACK_PEERS):
        row = jnp.concatenate([tail[:, j * CAP : (j + 1) * CAP], jnp.zeros((TAIL, LANES - CAP), F32)], axis=1)
        out_ref[j, BLOCK - TAIL :, :] = row.astype(BF16)


def pack(first, routes, ids, feats, cot):
    whole = lambda shape: pl.BlockSpec(shape, lambda i, f: (0,) * len(shape))
    return pl.pallas_call(
        pack_body,
        grid_spec=pltpu.PrefetchScalarGridSpec(
            num_scalar_prefetch=1,
            grid=(PEERS // PACK_PEERS,),
            in_specs=[whole((1, ROWS_DEV)), whole((1, ROWS_DEV)), whole((ROWS_DEV, D)), whole((ROWS_DEV, D))],
            out_specs=[
                pl.BlockSpec((PACK_PEERS, BLOCK, LANES), lambda i, f: (i, 0, 0)),
                whole((8, ROWS_DEV)),
            ],
            scratch_shapes=[pltpu.VMEM((8, ROWS_DEV), jnp.int32), pltpu.VMEM((16, ROWS_DEV), BF16)],
        ),
        out_shape=[
            jax.ShapeDtypeStruct((PEERS, BLOCK, LANES), BF16),
            jax.ShapeDtypeStruct((8, ROWS_DEV), jnp.int32),
        ],
        compiler_params=params_of(),
        name="pack",
    )(first, routes, ids, feats, cot)


def join_body(shards_ref, out_ref, scr):
    for n in range(NARROW):
        scr[n * SHARD : (n + 1) * SHARD, :] = shards_ref[n, :SHARD, :].astype(F32)
    out_ref[...] = scr[...].astype(BF16)


def join(shards):
    return pl.pallas_call(
        join_body,
        out_shape=jax.ShapeDtypeStruct((PROWS, D), BF16),
        scratch_shapes=[pltpu.VMEM((PROWS, D), F32)],
        compiler_params=params_of(),
        name="join",
    )(shards)


EXP_PEERS = 4
EXP_ROWS = EXP_PEERS * CAP
WIN = 2 * IMG_DEV


def columns(ref, half):
    parts = []
    for c in range(CHUNKS):
        r = (half * CHUNKS + c) * CAP
        parts.append(ref[:, r : r + CAP, :].reshape(EXP_ROWS, LANES))
    return jnp.concatenate(parts, axis=1)


def store_columns(ref, half, value):
    for c in range(CHUNKS):
        r = (half * CHUNKS + c) * CAP
        ref[:, r : r + CAP, :] = value[:, c * LANES : (c + 1) * LANES].reshape(EXP_PEERS, CAP, LANES)


def expert_body(got_ref, win_ref, w_ref, out_ref, z_ref, err_ref, code_ref):
    weights = lambda l: w_ref[l * D : (l + 1) * D, :]
    code_matrix = w_ref[LAYERS * D :, :]
    rows = EXP_PEERS * WIN
    image = lax.broadcasted_iota(jnp.int32, (rows, EXP_ROWS), 0) + 1
    key = jnp.concatenate(
        [
            jnp.where(v > 0.0, v + float(j * WIN), 0.0)
            for j in range(EXP_PEERS)
            for v in [got_ref[j, BLOCK - TAIL :, :CAP].astype(F32)]
        ],
        axis=1,
    )[0:1]
    hot = (key.astype(jnp.int32) == image).astype(F32).astype(BF16)
    code_rows = dot(hot, win_ref[...], 0, 0).astype(BF16)
    code_ref[...] = code_rows

    current = columns(got_ref, 0)
    slopes = []
    for l in range(LAYERS):
        z_ref[l] = current
        pre = dot(current, weights(l))
        if l == 0:
            pre = pre + dot(code_rows, code_matrix)
        s = 0.5 * jnp.tanh(0.5 * pre) + 0.5
        act = pre * s
        slopes.append(s + act * (1.0 - s))
        current = act.astype(BF16)
    store_columns(out_ref, 0, current)
    up = columns(got_ref, 1).astype(F32)
    for l in range(LAYERS - 1, -1, -1):
        err = (up * slopes[l]).astype(BF16)
        err_ref[l] = err
        up = dot(err, weights(l), 1, 1)
    store_columns(out_ref, 1, up.astype(BF16))
    code_back = dot(err, code_matrix, 1, 1).astype(BF16)
    sums = dot(hot, code_back)
    pad = jnp.zeros((IMG_DEV, LANES // 2 - CODE), F32)
    for j in range(EXP_PEERS):
        low = sums[j * WIN : j * WIN + IMG_DEV]
        high = sums[j * WIN + IMG_DEV : (j + 1) * WIN]
        out_ref[j, BLOCK - TAIL :, :] = jnp.concatenate([low, pad, high, pad], axis=1).astype(BF16)


def expert(got, window, weights):
    rows = PEERS * CAP
    return pl.pallas_call(
        expert_body,
        grid=(PEERS // EXP_PEERS,),
        in_specs=[
            pl.BlockSpec((EXP_PEERS, BLOCK, LANES), lambda i: (i, 0, 0)),
            pl.BlockSpec((EXP_PEERS * WIN, CODE), lambda i: (i, 0)),
            pl.BlockSpec((PROWS, D), lambda i: (0, 0)),
        ],
        out_specs=[
            pl.BlockSpec((EXP_PEERS, BLOCK, LANES), lambda i: (i, 0, 0)),
            pl.BlockSpec((LAYERS, EXP_ROWS, D), lambda i: (0, i, 0)),
            pl.BlockSpec((LAYERS, EXP_ROWS, D), lambda i: (0, i, 0)),
            pl.BlockSpec((EXP_ROWS, CODE), lambda i: (i, 0)),
        ],
        out_shape=[
            jax.ShapeDtypeStruct((PEERS, BLOCK, LANES), BF16),
            jax.ShapeDtypeStruct((LAYERS, rows, D), BF16),
            jax.ShapeDtypeStruct((LAYERS, rows, D), BF16),
            jax.ShapeDtypeStruct((rows, CODE), BF16),
        ],
        compiler_params=params_of(),
        name="expert",
    )(got, window, weights)


def grads_body(z_ref, err_ref, code_ref, out_ref, scr):
    l = pl.program_id(0)
    scr[pl.ds(pl.multiple_of(l * D, D), D), :] = dot(z_ref[0], err_ref[0], 0, 0)

    @pl.when(l == 0)
    def _():
        scr[LAYERS * D :, :] = dot(code_ref[...], err_ref[0], 0, 0)

    @pl.when(l == LAYERS - 1)
    def _():
        for n in range(NARROW):
            out_ref[n, :SHARD, :] = scr[n * SHARD : (n + 1) * SHARD, :].astype(BF16)
            out_ref[n, SHARD:, :] = jnp.zeros((SHARD_PAD - SHARD, D), BF16)


def grads(z, err, code):
    rows = PEERS * CAP
    return pl.pallas_call(
        grads_body,
        grid=(LAYERS,),
        in_specs=[
            pl.BlockSpec((1, rows, D), lambda i: (i, 0, 0)),
            pl.BlockSpec((1, rows, D), lambda i: (i, 0, 0)),
            pl.BlockSpec((rows, CODE), lambda i: (0, 0)),
        ],
        out_specs=pl.BlockSpec((NARROW, SHARD_PAD, D), lambda i: (0, 0, 0)),
        out_shape=jax.ShapeDtypeStruct((NARROW, SHARD_PAD, D), BF16),
        scratch_shapes=[pltpu.VMEM((PROWS, D), F32)],
        compiler_params=params_of(),
        name="grads",
    )(z, err, code)


UNPACK_ROWS = 256


def unpack_body(pos_ref, back_ref, out_ref, feat_ref):
    place = jnp.broadcast_to(pos_ref[0:1, :].astype(F32), (LANES, UNPACK_ROWS)).T
    place = place.astype(jnp.int32)
    lane = lax.broadcasted_iota(jnp.int32, (UNPACK_ROWS, LANES), 1)
    pick = jnp.concatenate(
        [(place == lane + b * LANES).astype(F32).astype(BF16) for b in range(PEERS * CAP // LANES)], axis=1
    )
    for half, dst in enumerate((out_ref, feat_ref)):
        parts = []
        for c in range(CHUNKS):
            r = (half * CHUNKS + c) * CAP
            parts.append(back_ref[:, r : r + CAP, :].reshape(PEERS * CAP, LANES))
        dst[...] = dot(pick, jnp.concatenate(parts, axis=1)).astype(BF16)


def unpack(pos, back):
    return pl.pallas_call(
        unpack_body,
        grid=(ROWS_DEV // UNPACK_ROWS,),
        in_specs=[
            pl.BlockSpec((8, UNPACK_ROWS), lambda i: (0, i)),
            pl.BlockSpec((PEERS, BLOCK, LANES), lambda i: (0, 0, 0)),
        ],
        out_specs=[pl.BlockSpec((UNPACK_ROWS, D), lambda i: (i, 0))] * 2,
        out_shape=[jax.ShapeDtypeStruct((ROWS_DEV, D), BF16)] * 2,
        compiler_params=params_of(),
        name="unpack",
    )(pos, back)


def exchange(values):
    return lax.all_to_all(values, "expert", split_axis=0, concat_axis=0, tiled=True)


def shifted(block, axis, distance):
    devices = range(lax.axis_size(axis))
    route = [((i - distance) % len(devices), i) for i in devices]
    return lax.ppermute(block, axis, route)


def body(feats, cotangent, routes, image_ids, codes, params):
    flat = lax.axis_index(("expert", "narrow"))
    first_image = (flat * IMG_DEV).astype(jnp.int32).reshape(1)
    shards = lax.all_gather(
        jnp.pad(params[0], ((0, SHARD_PAD - SHARD), (0, 0))), "narrow", axis=0, tiled=True
    ).reshape(NARROW, SHARD_PAD, D)
    packed, pos = pack(
        first_image, routes.reshape(1, ROWS_DEV), image_ids.reshape(1, ROWS_DEV), feats, cotangent
    )
    got = exchange(packed)
    weights = join(shards)
    start = lax.axis_index("narrow") * IMG_DEV
    ring = jnp.concatenate([codes, codes[:CAP]], axis=0)
    window = lax.dynamic_slice(ring, (start, 0), (PEERS * CAP, CODE))
    window = window.reshape(PEERS, CAP, CODE)[:, :WIN].reshape(PEERS * WIN, CODE)
    reply, z, err, code_rows = expert(got, window, weights)
    back = exchange(reply)
    terms = grads(z, err, code_rows)
    mine = lax.psum_scatter(
        terms.reshape(NARROW * SHARD_PAD, D), "narrow", scatter_dimension=0, tiled=True
    )
    param_grad = mine[None, :SHARD].astype(F32)
    sums = jnp.sum(back[:, BLOCK - TAIL :, :].astype(F32), axis=0)
    high = shifted(sums[:, LANES // 2 : LANES // 2 + CODE], ("expert", "narrow"), 1)
    out_rows, feat_grad = unpack(pos, back)
    return (out_rows, feat_grad, param_grad, sums[:, :CODE] + high)


def solution(mesh):
    rows = P(("expert", "narrow"), None)
    in_specs = (rows, rows, rows, P(("expert", "narrow")), P(), P("expert", "narrow", None))
    out_specs = (rows, rows, P("expert", "narrow", None), rows)
    return jax.shard_map(body, mesh=mesh, in_specs=in_specs, out_specs=out_specs, check_vma=False)
```

profile of v0, /device:TPU:96, one launch (start us, length us, event | category | flops | bytes accessed | tf_op | source)
XLA Modules:
  0.0 183.2 jit_solution(12227457128206610215)
XLA Ops:
  7.2 9.0 %pack.1 = (bf16[32,520,128]{2,1,0:T(8,128)(2,1)}, s32[8,1024]{1,0:T(8,128)}) custom-call(s32[1]{0:T(128)} %bitcast.first_ref, s32[1,1024]{1,0:T(1,128)} %bitcast.15, s32[1,1024]{1,0:T(1,128)} %bitcast.16, bf16[1024,512]{1,0:T(8,128)(2,1)} %feats_ref.1, bf16[1024,512]{1,0:T(8,128)(2,1)} %cot_ref.1), custom_call_target="tpu_custom_call" | custom-call | tf_op jit(solution)/shard_map/pack/pallas_call | solution.py:80
  16.1 0.0 copy-start
  16.1 0.0 copy-start.1
  16.1 0.0 slice-start
  16.1 7.6 %all-to-all-start = ((bf16[32,520,128]{2,1,0:T(8,128)(2,1)}), bf16[32,520,128]{2,1,0:T(8,128)(2,1)}, u32[]{:S(2)}, u32[]{:S(2)}) async-start(bf16[32,520,128]{2,1,0:T(8,128)(2,1)} %get-tuple-element.13), calls=%async_computation | async-start | bytes 8519680 | tf_op jit(solution)/shard_map/all_to_all | solution.py:274
  23.7 0.0 all-gather.2.cloned.1.call-start
  23.8 0.0 copy-done
  23.8 0.7 pad.4
  24.5 0.0 all-gather.2.cloned.1.call-update
  24.5 0.0 copy-done.1
  24.5 0.0 slice-done
  24.6 0.2 fusion
  24.7 0.4 reshape.34
  25.1 1.1 copy.10
  26.2 43.1 %all-gather.2.cloned.1.call-done = bf16[2112,512]{1,0:T(8,128)(2,1)} async-done(((bf16[264,512]{1,0:T(8,128)(2,1)}), bf16[2112,512]{1,0:T(8,128)(2,1)}) %all-gather.2.cloned.1.call-update) | async-done | bytes 2162704 | tf_op jit(solution)/shard_map/all_gather | solution.py:286
  69.3 3.6 %join.1.w_ref = bf16[2096,512]{1,0:T(8,128)(2,1)} custom-call(bf16[8,264,512]{2,1,0:T(8,128)(2,1)} %bitcast.11), custom_call_target="tpu_custom_call" | custom-call | tf_op jit(solution)/shard_map/join/pallas_call | solution.py:108
  72.9 5.1 %all-to-all-done.got_ref = bf16[32,520,128]{2,1,0:T(8,128)(2,1)} async-done(((bf16[32,520,128]{2,1,0:T(8,128)(2,1)}), bf16[32,520,128]{2,1,0:T(8,128)(2,1)}, u32[]{:S(2)}, u32[]{:S(2)}) %all-to-all-start) | async-done | bytes 4259872 | tf_op jit(solution)/shard_map/all_to_all | solution.py:274
  78.0 24.0 %expert.1 = (bf16[32,520,128]{2,1,0:T(8,128)(2,1)}, bf16[4,2048,512]{2,1,0:T(8,128)(2,1)}, bf16[4,2048,512]{2,1,0:T(8,128)(2,1)}, bf16[2048,48]{1,0:T(8,128)(2,1)}) custom-call(bf16[32,520,128]{2,1,0:T(8,128)(2,1)} %all-to-all-done.got_ref, bf16[512,48]{1,0:T(8,128)(2,1)} %bitcast.13, bf16[2096,512]{1,0:T(8,128)(2,1)} %join.1.w_ref), custom_call_target="tpu_custom_call" | custom-call | tf_op jit(solution)/shard_map/expert/pallas_call | solution.py:182
  102.1 4.9 %all-to-all-start.1 = ((bf16[32,520,128]{2,1,0:T(8,128)(2,1)}), bf16[32,520,128]{2,1,0:T(8,128)(2,1)}, u32[]{:S(2)}, u32[]{:S(2)}) async-start(bf16[32,520,128]{2,1,0:T(8,128)(2,1)} %get-tuple-element.14), calls=%async_computation.1 | async-start | bytes 8519680 | tf_op jit(solution)/shard_map/all_to_all | solution.py:274
  106.9 0.0 reduce-scatter.2.cloned.1.call-start
  107.0 10.8 %grads.1 = bf16[8,264,512]{2,1,0:T(8,128)(2,1)} custom-call(bf16[4,2048,512]{2,1,0:T(8,128)(2,1)} %get-tuple-element.17.z_ref, bf16[4,2048,512]{2,1,0:T(8,128)(2,1)} %get-tuple-element.18.err_ref, bf16[2048,48]{1,0:T(8,128)(2,1)} %get-tuple-element.19.code_ref), custom_call_target="tpu_custom_call" | custom-call | tf_op jit(solution)/shard_map/grads/pallas_call | solution.py:224
  117.8 0.0 reduce-scatter.2.cloned.1.call-update
  117.8 43.5 %all-to-all-done.1.back_ref = bf16[32,520,128]{2,1,0:T(8,128)(2,1)} async-done(((bf16[32,520,128]{2,1,0:T(8,128)(2,1)}), bf16[32,520,128]{2,1,0:T(8,128)(2,1)}, u32[]{:S(2)}, u32[]{:S(2)}) %all-to-all-start.1) | async-done | bytes 4259872 | tf_op jit(solution)/shard_map/all_to_all | solution.py:274
  161.2 0.9 convert_reduce_fusion
  162.1 0.1 slice.23
  162.2 3.2 %collective-permute-start = (f32[8,48]{1,0:T(8,128)S(1)}, f32[8,48]{1,0:T(8,128)S(1)}, u32[]{:S(2)}, u32[]{:S(2)}) collective-permute-start(f32[8,48]{1,0:T(8,128)S(1)} %slice.23), channel_id=1, source_target_pairs={{255,0},{0,1},{1,2},{2,3},{3,4},{4,5},{5,6},{6,7},{7,8},{8,9},{9,1... | collective-permute-start | bytes 4616 | tf_op jit(solution)/shard_map/ppermute | solution.py:280
  165.4 8.2 %unpack.1 = (bf16[1024,512]{1,0:T(8,128)(2,1)}, bf16[1024,512]{1,0:T(8,128)(2,1)}) custom-call(s32[8,1024]{1,0:T(8,128)} %get-tuple-element.12.pos_ref, bf16[32,520,128]{2,1,0:T(8,128)(2,1)} %all-to-all-done.1.back_ref), custom_call_target="tpu_custom_call" | custom-call | tf_op jit(solution)/shard_map/unpack/pallas_call | solution.py:259
  173.6 0.0 collective-permute-done
  173.6 0.6 slice_add_fusion
  174.2 0.0 reduce-scatter.2.cloned.1.call-done
  174.2 1.0 slice_convert_fusion
  175.2 1.2 reshape.38
Async XLA Ops:
  16.1 7.6 %copy-start = (bf16[1,262,512]{2,1,0:T(8,128)(2,1)S(1)}, bf16[1,262,512]{2,1,0:T(8,128)(2,1)}, u32[]{:S(2)}) copy-start(bf16[1,262,512]{2,1,0:T(8,128)(2,1)} %param.11) | copy-start | bytes 804868
  16.1 8.4 %copy-start.1 = (bf16[2048,48]{0,1:T(8,128)(2,1)S(1)}, bf16[2048,48]{0,1:T(8,128)(2,1)}, u32[]{:S(2)}) copy-start(bf16[2048,48]{0,1:T(8,128)(2,1)} %param.10) | copy-start | bytes 589828
  16.1 8.4 %slice-start = ((bf16[2048,48]{0,1:T(8,128)(2,1)}), bf16[64,48]{0,1:T(8,128)(2,1)S(1)}, s32[]{:S(2)}) async-start(bf16[2048,48]{0,1:T(8,128)(2,1)} %param.10), calls=%async_computation.5 | async-start | bytes 24576 | tf_op jit(solution)/shard_map/slice | solution.py:295
  16.1 61.9 %all-to-all-start = ((bf16[32,520,128]{2,1,0:T(8,128)(2,1)}), bf16[32,520,128]{2,1,0:T(8,128)(2,1)}, u32[]{:S(2)}, u32[]{:S(2)}) async-start(bf16[32,520,128]{2,1,0:T(8,128)(2,1)} %get-tuple-element.13), calls=%async_computation | async-start | bytes 8519680 | tf_op jit(solution)/shard_map/all_to_all | solution.py:274
  23.7 45.6 %all-gather.2.cloned.1.call-start = ((), (), s32[]{:S(2)}) async-start(), calls=%async_computation.3 | async-start | bytes 2433024 | tf_op jit(solution)/shard_map/all_gather | solution.py:286
  102.1 59.2 %all-to-all-start.1 = ((bf16[32,520,128]{2,1,0:T(8,128)(2,1)}), bf16[32,520,128]{2,1,0:T(8,128)(2,1)}, u32[]{:S(2)}, u32[]{:S(2)}) async-start(bf16[32,520,128]{2,1,0:T(8,128)(2,1)} %get-tuple-element.14), calls=%async_computation.1 | async-start | bytes 8519680 | tf_op jit(solution)/shard_map/all_to_all | solution.py:274
  106.9 67.2 %reduce-scatter.2.cloned.1.call-start = ((), (), s32[]{:S(2)}) async-start(), calls=%async_computation.4 | async-start | bytes 2433024 | tf_op jit(solution)/shard_map/reduce_scatter | solution.py:301
  162.2 11.4 %collective-permute-start = (f32[8,48]{1,0:T(8,128)S(1)}, f32[8,48]{1,0:T(8,128)S(1)}, u32[]{:S(2)}, u32[]{:S(2)}) collective-permute-start(f32[8,48]{1,0:T(8,128)S(1)} %slice.23), channel_id=1, source_target_pairs={{255,0},{0,1},{1,2},{2,3},{3,4},{4,5},{5,6},{6,7},{7,8},{8,9},{9,1... | collective-permute-start | bytes 4616 | tf_op jit(solution)/shard_map/ppermute | solution.py:280
Sparse Core Ops, SparseCore 0:
  26.9 42.3 all-gather.1
  117.9 43.5 reduce-scatter.1
where the time goes:
time: 184 us; the launch traced here: 183 us
  waiting for transfers between devices  91.7 us (50%)
  Pallas kernels  55.6 us (30%)
  starting transfers between devices  15.7 us (9%)
  between operations  14.1 us (8%)
  local copies, waits for them, and re-layouts  3.44 us (2%)
  other arithmetic  2.67 us (1%)
    all_to_all x2, waiting for transfers between devices, exchange(): lax.all_to_all(values, 'expert', split_axis=0, concat_axis=0, tiled=True)  48.6 us
    all_gather x1, waiting for transfers between devices, body(): lax.all_gather(jnp.pad(params[0], ((0, SHARD_PAD - SHARD), (0, 0))), 'nar...  43.1 us
    pallas_call x1, Pallas kernels, expert(): pl.pallas_call(expert_body, grid=(PEERS // EXP_PEERS,), in_specs=[pl.Bloc...  24 us
    all_to_all x2, starting transfers between devices, exchange(): lax.all_to_all(values, 'expert', split_axis=0, concat_axis=0, tiled=True)  12.4 us
    pallas_call x1, Pallas kernels, grads(): pl.pallas_call(grads_body, grid=(LAYERS,), in_specs=[pl.BlockSpec((1, row...  10.8 us
    pallas_call x1, Pallas kernels, pack(): pl.pallas_call(pack_body, grid_spec=pltpu.PrefetchScalarGridSpec(num_scal...  8.97 us
    pallas_call x1, Pallas kernels, unpack(): pl.pallas_call(unpack_body, grid=(ROWS_DEV // UNPACK_ROWS,), in_specs=[pl...  8.16 us
  transfers between devices with their start and end apart: 5, of which 3 were waited for; matrix products, arithmetic and copies ran while one was open for 2% of the time, Pallas kernels for 12%

commit v1 on v0

--- a/solution.py
+++ b/solution.py
@@ -98,23 +98,35 @@
     )(first, routes, ids, feats, cot)
 
 
-def join_body(shards_ref, out_ref, scr):
+HOPS = (0, -1, 1, -2, 2, -3, 3, -4)
+
+
+def join_body(narrow_ref, *refs):
+    shard_refs, (out_ref, order, scr) = refs[:NARROW], refs[NARROW:]
+    for hop, ref in zip(HOPS, shard_refs):
+        order[(narrow_ref[0] + hop + NARROW) % NARROW] = ref[...]
     for n in range(NARROW):
-        scr[n * SHARD : (n + 1) * SHARD, :] = shards_ref[n, :SHARD, :].astype(F32)
+        scr[n * SHARD : (n + 1) * SHARD, :] = order[n, :SHARD, :].astype(F32)
     out_ref[...] = scr[...].astype(BF16)
 
 
-def join(shards):
+def join(narrow, shards):
     return pl.pallas_call(
         join_body,
+        grid_spec=pltpu.PrefetchScalarGridSpec(
+            num_scalar_prefetch=1,
+            grid=(1,),
+            in_specs=[pl.BlockSpec((SHARD_PAD, D), lambda i, n: (0, 0))] * NARROW,
+            out_specs=pl.BlockSpec((PROWS, D), lambda i, n: (0, 0)),
+            scratch_shapes=[pltpu.VMEM((NARROW, SHARD_PAD, D), BF16), pltpu.VMEM((PROWS, D), F32)],
+        ),
         out_shape=jax.ShapeDtypeStruct((PROWS, D), BF16),
-        scratch_shapes=[pltpu.VMEM((PROWS, D), F32)],
         compiler_params=params_of(),
         name="join",
-    )(shards)
-
-
-EXP_PEERS = 4
+    )(narrow, *shards)
+
+
+EXP_PEERS = 8
 EXP_ROWS = EXP_PEERS * CAP
 WIN = 2 * IMG_DEV
 
@@ -204,7 +216,8 @@
     )(got, window, weights)
 
 
-def grads_body(z_ref, err_ref, code_ref, out_ref, scr):
+def grads_body(narrow_ref, z_ref, err_ref, code_ref, *refs):
+    out_refs, (scr, order) = refs[:NARROW], refs[NARROW:]
     l = pl.program_id(0)
     scr[pl.ds(pl.multiple_of(l * D, D), D), :] = dot(z_ref[0], err_ref[0], 0, 0)
 
@@ -215,26 +228,31 @@
     @pl.when(l == LAYERS - 1)
     def _():
         for n in range(NARROW):
-            out_ref[n, :SHARD, :] = scr[n * SHARD : (n + 1) * SHARD, :].astype(BF16)
-            out_ref[n, SHARD:, :] = jnp.zeros((SHARD_PAD - SHARD, D), BF16)
-
-
-def grads(z, err, code):
+            order[n, :SHARD, :] = scr[n * SHARD : (n + 1) * SHARD, :].astype(BF16)
+            order[n, SHARD:, :] = jnp.zeros((SHARD_PAD - SHARD, D), BF16)
+        for k, ref in enumerate(out_refs):
+            ref[...] = order[(narrow_ref[0] + k) % NARROW]
+
+
+def grads(narrow, z, err, code):
     rows = PEERS * CAP
     return pl.pallas_call(
         grads_body,
-        grid=(LAYERS,),
-        in_specs=[
-            pl.BlockSpec((1, rows, D), lambda i: (i, 0, 0)),
-            pl.BlockSpec((1, rows, D), lambda i: (i, 0, 0)),
-            pl.BlockSpec((rows, CODE), lambda i: (0, 0)),
-        ],
-        out_specs=pl.BlockSpec((NARROW, SHARD_PAD, D), lambda i: (0, 0, 0)),
-        out_shape=jax.ShapeDtypeStruct((NARROW, SHARD_PAD, D), BF16),
-        scratch_shapes=[pltpu.VMEM((PROWS, D), F32)],
+        grid_spec=pltpu.PrefetchScalarGridSpec(
+            num_scalar_prefetch=1,
+            grid=(LAYERS,),
+            in_specs=[
+                pl.BlockSpec((1, rows, D), lambda i, n: (i, 0, 0)),
+                pl.BlockSpec((1, rows, D), lambda i, n: (i, 0, 0)),
+                pl.BlockSpec((rows, CODE), lambda i, n: (0, 0)),
+            ],
+            out_specs=[pl.BlockSpec((SHARD_PAD, D), lambda i, n: (0, 0))] * NARROW,
+            scratch_shapes=[pltpu.VMEM((PROWS, D), F32), pltpu.VMEM((NARROW, SHARD_PAD, D), BF16)],
+        ),
+        out_shape=[jax.ShapeDtypeStruct((SHARD_PAD, D), BF16)] * NARROW,
         compiler_params=params_of(),
         name="grads",
-    )(z, err, code)
+    )(narrow, z, err, code)
 
 
 UNPACK_ROWS = 256
@@ -280,28 +298,50 @@
     return lax.ppermute(block, axis, route)
 
 
+def ring_gather(own):
+    got = [own]
+    ahead = behind = own
+    for step in range(1, NARROW // 2 + 1):
+        ahead = shifted(ahead, "narrow", 1)
+        got.append(ahead)
+        if step < NARROW // 2:
+            behind = shifted(behind, "narrow", -1)
+            got.append(behind)
+    return got
+
+
+def ring_reduce(terms):
+    add = lambda a, b: a.astype(F32) + b.astype(F32)
+    half = NARROW // 2
+    ahead, behind = terms[half], terms[half + 1]
+    for step in range(half):
+        ahead = shifted(ahead, "narrow", 1)
+        if step > 0:
+            behind = shifted(behind, "narrow", -1)
+        if step < half - 1:
+            ahead = add(ahead, terms[half - 1 - step]).astype(BF16)
+            if step > 0:
+                behind = add(behind, terms[half + 1 + step]).astype(BF16)
+    return add(ahead, behind) + terms[0].astype(F32)
+
+
 def body(feats, cotangent, routes, image_ids, codes, params):
     flat = lax.axis_index(("expert", "narrow"))
     first_image = (flat * IMG_DEV).astype(jnp.int32).reshape(1)
-    shards = lax.all_gather(
-        jnp.pad(params[0], ((0, SHARD_PAD - SHARD), (0, 0))), "narrow", axis=0, tiled=True
-    ).reshape(NARROW, SHARD_PAD, D)
+    narrow = lax.axis_index("narrow").astype(jnp.int32)
     packed, pos = pack(
         first_image, routes.reshape(1, ROWS_DEV), image_ids.reshape(1, ROWS_DEV), feats, cotangent
     )
     got = exchange(packed)
-    weights = join(shards)
-    start = lax.axis_index("narrow") * IMG_DEV
+    shards = ring_gather(jnp.pad(params[0], ((0, SHARD_PAD - SHARD), (0, 0))))
+    weights = join(narrow.reshape(1), shards)
     ring = jnp.concatenate([codes, codes[:CAP]], axis=0)
-    window = lax.dynamic_slice(ring, (start, 0), (PEERS * CAP, CODE))
+    window = lax.dynamic_slice(ring, (narrow * IMG_DEV, 0), (PEERS * CAP, CODE))
     window = window.reshape(PEERS, CAP, CODE)[:, :WIN].reshape(PEERS * WIN, CODE)
     reply, z, err, code_rows = expert(got, window, weights)
     back = exchange(reply)
-    terms = grads(z, err, code_rows)
-    mine = lax.psum_scatter(
-        terms.reshape(NARROW * SHARD_PAD, D), "narrow", scatter_dimension=0, tiled=True
-    )
-    param_grad = mine[None, :SHARD].astype(F32)
+    mine = ring_reduce(grads(narrow.reshape(1), z, err, code_rows))
+    param_grad = mine[None, :SHARD]
     sums = jnp.sum(back[:, BLOCK - TAIL :, :].astype(F32), axis=0)
     high = shifted(sums[:, LANES // 2 : LANES // 2 + CODE], ("expert", "narrow"), 1)
     out_rows, feat_grad = unpack(pos, back)

time: 184 us -> 164 us (0.89)
  waiting for transfers between devices: 91.7 us -> 57.7 us
  starting transfers between devices: 15.7 us -> 44.6 us
  between operations: 14.1 us -> 0.8 us
  Pallas kernels: 55.6 us -> 49.9 us
  other arithmetic: 2.67 us -> 6.85 us
    all_gather x1 -> x0, waiting for transfers between devices: 43.1 us -> none  [body(): lax.all_gather(jnp.pad(params[0], ((0, SHARD_PAD - SHARD), (0, 0))), 'nar...]
    ppermute x1 -> x15, waiting for transfers between devices: 0.01 us -> 32.2 us  [shifted(): return lax.ppermute(block, axis, route)]
    ppermute x1 -> x15, starting transfers between devices: 3.2 us -> 31.9 us  [shifted(): return lax.ppermute(block, axis, route)]
    all_to_all x2, waiting for transfers between devices: 48.6 us -> 25.4 us  [exchange(): lax.all_to_all(values, 'expert', split_axis=0, concat_axis=0, tiled=True)]
    pallas_call x1, Pallas kernels: 24 us -> 18.3 us  [expert(): pl.pallas_call(expert_body, grid=(PEERS // EXP_PEERS,), in_specs=[pl.Bloc...]
    convert_element_type x1 -> x5, other arithmetic: 1 us -> 5.1 us  [the longest x3 3.06 us: ring_reduce(): ahead = add(ahead, terms[half - 1 - step]).astype(BF16)]
    unnamed x4 -> x23, local copies, waits for them, and re-layouts: 0.01 us -> 2.06 us
  transfers between devices with their start and end apart: 5 -> 17, of which waited for: 3 -> 9; matrix products, arithmetic and copies ran while one was open for 2% -> 6% of each run, Pallas kernels for 12% -> 14%
where the time goes in v1:
time: 164 us; the launch traced here: 163 us
  waiting for transfers between devices  57.7 us (35%)
  Pallas kernels  49.9 us (30%)
  starting transfers between devices  44.6 us (27%)
  other arithmetic  6.85 us (4%)
  local copies, waits for them, and re-layouts  3.61 us (2%)
    ppermute x15, waiting for transfers between devices, shifted(): return lax.ppermute(block, axis, route)  32.2 us
    ppermute x15, starting transfers between devices, shifted(): return lax.ppermute(block, axis, route)  31.9 us
    all_to_all x2, waiting for transfers between devices, exchange(): lax.all_to_all(values, 'expert', split_axis=0, concat_axis=0, tiled=True)  25.4 us
    pallas_call x1, Pallas kernels, expert(): pl.pallas_call(expert_body, grid=(PEERS // EXP_PEERS,), in_specs=[pl.Bloc...  18.3 us
    all_to_all x2, starting transfers between devices, exchange(): lax.all_to_all(values, 'expert', split_axis=0, concat_axis=0, tiled=True)  12.6 us
    pallas_call x1, Pallas kernels, grads(): pl.pallas_call(grads_body, grid_spec=pltpu.PrefetchScalarGridSpec(num_sca...  10.9 us
    pallas_call x1, Pallas kernels, pack(): pl.pallas_call(pack_body, grid_spec=pltpu.PrefetchScalarGridSpec(num_scal...  8.92 us
    pallas_call x1, Pallas kernels, unpack(): pl.pallas_call(unpack_body, grid=(ROWS_DEV // UNPACK_ROWS,), in_specs=[pl...  8.15 us
  transfers between devices with their start and end apart: 17, of which 9 were waited for; matrix products, arithmetic and copies ran while one was open for 6% of the time, Pallas kernels for 14%

profile of v1, /device:TPU:96, one launch (start us, length us, event | category | flops | bytes accessed | tf_op | source)
XLA Modules:
  0.0 163.4 jit_solution(1835587412615884017)
XLA Ops:
  0.6 8.9 %pack.1 = (bf16[32,520,128]{2,1,0:T(8,128)(2,1)}, s32[8,1024]{1,0:T(8,128)}) custom-call(s32[1]{0:T(128)} %bitcast.first_ref, s32[1,1024]{1,0:T(1,128)} %bitcast.14, s32[1,1024]{1,0:T(1,128)} %bitcast.15, bf16[1024,512]{1,0:T(8,128)(2,1)} %feats_ref.1, bf16[1024,512]{1,0:T(8,128)(2,1)} %cot_ref.1), custom_call_target="tpu_custom_call" | custom-call | tf_op jit(solution)/shard_map/pack/pallas_call | solution.py:80
  9.6 7.6 %all-to-all-start = ((bf16[32,520,128]{2,1,0:T(8,128)(2,1)}), bf16[32,520,128]{2,1,0:T(8,128)(2,1)}, u32[]{:S(2)}, u32[]{:S(2)}) async-start(bf16[32,520,128]{2,1,0:T(8,128)(2,1)} %get-tuple-element.21), calls=%async_computation | async-start | bytes 8519680 | tf_op jit(solution)/shard_map/all_to_all | solution.py:292
  17.2 0.0 copy-done.8
  17.2 0.0 copy-start
  17.2 3.2 %collective-permute-start = (bf16[264,512]{1,0:T(8,128)(2,1)S(1)}, bf16[264,512]{1,0:T(8,128)(2,1)S(1)}, u32[]{:S(2)}, u32[]{:S(2)}) collective-permute-start(bf16[264,512]{1,0:T(8,128)(2,1)S(1)} %pad.4.refs_0_), channel_id=1, source_target_pairs={{7,0},{0,1},{1,2},{2,3},{3,4},{4,5},{5,6},{6,7},{15,8},{8,9},{9,10... | collective-permute-start | bytes 811016 | tf_op jit(solution)/shard_map/ppermute | solution.py:298
  20.4 0.0 collective-permute-start.1
  20.4 6.1 %collective-permute-done.refs_1_ = bf16[264,512]{1,0:T(8,128)(2,1)S(1)} collective-permute-done((bf16[264,512]{1,0:T(8,128)(2,1)S(1)}, bf16[264,512]{1,0:T(8,128)(2,1)S(1)}, u32[]{:S(2)}, u32[]{:S(2)}) %collective-permute-start) | collective-permute-done | bytes 270368 | tf_op jit(solution)/shard_map/ppermute | solution.py:298
  26.5 3.7 %collective-permute-start.2 = (bf16[264,512]{1,0:T(8,128)(2,1)S(1)}, bf16[264,512]{1,0:T(8,128)(2,1)S(1)}, u32[]{:S(2)}, u32[]{:S(2)}) collective-permute-start(bf16[264,512]{1,0:T(8,128)(2,1)S(1)} %collective-permute-done.refs_1_), channel_id=1, source_target_pairs={{7,0},{0,1},{1,2},{2,3},{3,4},{4,5},{5,6},{6,7},{15,8},{8,9},{9,10... | collective-permute-start | bytes 811016 | tf_op jit(solution)/shard_map/ppermute | solution.py:298
  30.2 0.0 collective-permute-done.1.refs_2_
  30.2 0.0 collective-permute-start.3
  30.2 5.4 %collective-permute-done.2.refs_3_ = bf16[264,512]{1,0:T(8,128)(2,1)S(1)} collective-permute-done((bf16[264,512]{1,0:T(8,128)(2,1)S(1)}, bf16[264,512]{1,0:T(8,128)(2,1)S(1)}, u32[]{:S(2)}, u32[]{:S(2)}) %collective-permute-start.2) | collective-permute-done | bytes 270368 | tf_op jit(solution)/shard_map/ppermute | solution.py:298
  35.6 3.7 %collective-permute-start.4 = (bf16[264,512]{1,0:T(8,128)(2,1)S(1)}, bf16[264,512]{1,0:T(8,128)(2,1)S(1)}, u32[]{:S(2)}, u32[]{:S(2)}) collective-permute-start(bf16[264,512]{1,0:T(8,128)(2,1)S(1)} %collective-permute-done.2.refs_3_), channel_id=1, source_target_pairs={{7,0},{0,1},{1,2},{2,3},{3,4},{4,5},{5,6},{6,7},{15,8},{8,9},{9,10... | collective-permute-start | bytes 811016 | tf_op jit(solution)/shard_map/ppermute | solution.py:298
  39.3 0.0 collective-permute-done.3.refs_4_
  39.3 0.0 collective-permute-start.5
  39.3 4.6 %collective-permute-done.4.refs_5_ = bf16[264,512]{1,0:T(8,128)(2,1)S(1)} collective-permute-done((bf16[264,512]{1,0:T(8,128)(2,1)S(1)}, bf16[264,512]{1,0:T(8,128)(2,1)S(1)}, u32[]{:S(2)}, u32[]{:S(2)}) %collective-permute-start.4) | collective-permute-done | bytes 270368 | tf_op jit(solution)/shard_map/ppermute | solution.py:298
  43.9 3.7 %collective-permute-start.6 = (bf16[264,512]{1,0:T(8,128)(2,1)S(1)}, bf16[264,512]{1,0:T(8,128)(2,1)S(1)}, u32[]{:S(2)}, u32[]{:S(2)}) collective-permute-start(bf16[264,512]{1,0:T(8,128)(2,1)S(1)} %collective-permute-done.4.refs_5_), channel_id=1, source_target_pairs={{7,0},{0,1},{1,2},{2,3},{3,4},{4,5},{5,6},{6,7},{15,8},{8,9},{9,10... | collective-permute-start | bytes 811016 | tf_op jit(solution)/shard_map/ppermute | solution.py:298
  47.6 0.0 copy-done.10
  47.6 0.0 slice-done
  47.6 0.2 fusion
  47.8 0.4 reshape.30
  48.2 1.1 copy.11
  49.3 0.0 collective-permute-done.5.refs_6_
  49.3 2.3 %collective-permute-done.6.refs_7_ = bf16[264,512]{1,0:T(8,128)(2,1)S(1)} collective-permute-done((bf16[264,512]{1,0:T(8,128)(2,1)S(1)}, bf16[264,512]{1,0:T(8,128)(2,1)S(1)}, u32[]{:S(2)}, u32[]{:S(2)}) %collective-permute-start.6) | collective-permute-done | bytes 270368 | tf_op jit(solution)/shard_map/ppermute | solution.py:298
  51.6 0.0 copy-done
  51.6 0.0 copy-done.1
  51.6 0.0 copy-done.2
  51.6 0.0 copy-done.3
  51.6 0.0 copy-done.4
  51.6 0.0 copy-done.5
  51.6 0.0 copy-done.6
  51.6 0.7 copy-done.7
  52.3 3.7 %join.1.w_ref = bf16[2096,512]{1,0:T(8,128)(2,1)} custom-call(s32[1]{0:T(128)} %bitcast.4.narrow_ref, bf16[264,512]{1,0:T(8,128)(2,1)} %copy-done, bf16[264,512]{1,0:T(8,128)(2,1)} %copy-done.1, bf16[264,512]{1,0:T(8,128)(2,1)} %copy-done.2, bf16[264,512]{1,0:T(8,128)(2,1)} %copy-done.3, bf16[264,512]{1,0:T(8,128)(2,1)} %copy-done.4, ...), custom_call_target="tpu_custom_call" | custom-call | tf_op jit(solution)/shard_map/join/pallas_call | solution.py:114
  56.0 15.5 %all-to-all-done.got_ref = bf16[32,520,128]{2,1,0:T(8,128)(2,1)} async-done(((bf16[32,520,128]{2,1,0:T(8,128)(2,1)}), bf16[32,520,128]{2,1,0:T(8,128)(2,1)}, u32[]{:S(2)}, u32[]{:S(2)}) %all-to-all-start) | async-done | bytes 4259872 | tf_op jit(solution)/shard_map/all_to_all | solution.py:292
  71.5 18.3 %expert.1 = (bf16[32,520,128]{2,1,0:T(8,128)(2,1)}, bf16[4,2048,512]{2,1,0:T(8,128)(2,1)}, bf16[4,2048,512]{2,1,0:T(8,128)(2,1)}, bf16[2048,48]{1,0:T(8,128)(2,1)}) custom-call(bf16[32,520,128]{2,1,0:T(8,128)(2,1)} %all-to-all-done.got_ref, bf16[512,48]{1,0:T(8,128)(2,1)} %bitcast.12, bf16[2096,512]{1,0:T(8,128)(2,1)} %join.1.w_ref), custom_call_target="tpu_custom_call" | custom-call | tf_op jit(solution)/shard_map/expert/pallas_call | solution.py:194
  89.8 5.0 %all-to-all-start.1 = ((bf16[32,520,128]{2,1,0:T(8,128)(2,1)}), bf16[32,520,128]{2,1,0:T(8,128)(2,1)}, u32[]{:S(2)}, u32[]{:S(2)}) async-start(bf16[32,520,128]{2,1,0:T(8,128)(2,1)} %get-tuple-element.22), calls=%async_computation.1 | async-start | bytes 8519680 | tf_op jit(solution)/shard_map/all_to_all | solution.py:292
  94.8 10.9 %grads.1 = (bf16[264,512]{1,0:T(8,128)(2,1)}, bf16[264,512]{1,0:T(8,128)(2,1)}, bf16[264,512]{1,0:T(8,128)(2,1)}, bf16[264,512]{1,0:T(8,128)(2,1)}, bf16[264,512...) custom-call(s32[1]{0:T(128)} %bitcast.4.narrow_ref, ...), custom_call_target="tpu_custom_call" | custom-call | tf_op jit(solution)/shard_map/grads/pallas_call | solution.py:239
  105.7 3.1 %collective-permute-start.7 = (bf16[264,512]{1,0:T(8,128)(2,1)}, bf16[264,512]{1,0:T(8,128)(2,1)S(1)}, u32[]{:S(2)}, u32[]{:S(2)}) collective-permute-start(bf16[264,512]{1,0:T(8,128)(2,1)} %get-tuple-element.28), channel_id=1, source_target_pairs={{7,0},{0,1},{1,2},{2,3},{3,4},{4,5},{5,6},{6,7},{15,8},{8,9},{9,10... | collective-permute-start | bytes 811016 | tf_op jit(solution)/shard_map/ppermute | solution.py:298
  108.9 0.0 collective-permute-start.11
  108.9 6.3 %collective-permute-done.7 = bf16[264,512]{1,0:T(8,128)(2,1)S(1)} collective-permute-done((bf16[264,512]{1,0:T(8,128)(2,1)}, bf16[264,512]{1,0:T(8,128)(2,1)S(1)}, u32[]{:S(2)}, u32[]{:S(2)}) %collective-permute-start.7) | collective-permute-done | bytes 270368 | tf_op jit(solution)/shard_map/ppermute | solution.py:298
  115.2 1.0 add_convert_fusion.4
  116.2 3.7 %collective-permute-start.8 = (bf16[264,512]{1,0:T(8,128)(2,1)S(1)}, bf16[264,512]{1,0:T(8,128)(2,1)S(1)}, u32[]{:S(2)}, u32[]{:S(2)}) collective-permute-start(bf16[264,512]{1,0:T(8,128)(2,1)S(1)} %add_convert_fusion.4), channel_id=1, source_target_pairs={{7,0},{0,1},{1,2},{2,3},{3,4},{4,5},{5,6},{6,7},{15,8},{8,9},{9,10... | collective-permute-start | bytes 811016 | tf_op jit(solution)/shard_map/ppermute | solution.py:298
  119.9 0.0 collective-permute-done.11
  119.9 1.0 add_convert_fusion.1
  120.9 0.1 collective-permute-start.12
  121.0 4.2 %collective-permute-done.8 = bf16[264,512]{1,0:T(8,128)(2,1)S(1)} collective-permute-done((bf16[264,512]{1,0:T(8,128)(2,1)S(1)}, bf16[264,512]{1,0:T(8,128)(2,1)S(1)}, u32[]{:S(2)}, u32[]{:S(2)}) %collective-permute-start.8) | collective-permute-done | bytes 270368 | tf_op jit(solution)/shard_map/ppermute | solution.py:298
  125.1 1.0 add_convert_fusion.3
  126.2 3.8 %collective-permute-start.9 = (bf16[264,512]{1,0:T(8,128)(2,1)S(1)}, bf16[264,512]{1,0:T(8,128)(2,1)S(1)}, u32[]{:S(2)}, u32[]{:S(2)}) collective-permute-start(bf16[264,512]{1,0:T(8,128)(2,1)S(1)} %add_convert_fusion.3), channel_id=1, source_target_pairs={{7,0},{0,1},{1,2},{2,3},{3,4},{4,5},{5,6},{6,7},{15,8},{8,9},{9,10... | collective-permute-start | bytes 811016 | tf_op jit(solution)/shard_map/ppermute | solution.py:298
  129.9 0.0 collective-permute-done.12
  129.9 1.0 add_convert_fusion
  131.0 0.1 collective-permute-start.13
  131.0 3.3 %collective-permute-done.9 = bf16[264,512]{1,0:T(8,128)(2,1)S(1)} collective-permute-done((bf16[264,512]{1,0:T(8,128)(2,1)S(1)}, bf16[264,512]{1,0:T(8,128)(2,1)S(1)}, u32[]{:S(2)}, u32[]{:S(2)}) %collective-permute-start.9) | collective-permute-done | bytes 270368 | tf_op jit(solution)/shard_map/ppermute | solution.py:298
  134.4 1.0 add_convert_fusion.2
  135.4 3.8 %collective-permute-start.10 = (bf16[264,512]{1,0:T(8,128)(2,1)S(1)}, bf16[264,512]{1,0:T(8,128)(2,1)S(1)}, u32[]{:S(2)}, u32[]{:S(2)}) collective-permute-start(bf16[264,512]{1,0:T(8,128)(2,1)S(1)} %add_convert_fusion.2), channel_id=1, source_target_pairs={{7,0},{0,1},{1,2},{2,3},{3,4},{4,5},{5,6},{6,7},{15,8},{8,9},{9,10... | collective-permute-start | bytes 811016 | tf_op jit(solution)/shard_map/ppermute | solution.py:298
  139.2 9.9 %all-to-all-done.1.back_ref = bf16[32,520,128]{2,1,0:T(8,128)(2,1)} async-done(((bf16[32,520,128]{2,1,0:T(8,128)(2,1)}), bf16[32,520,128]{2,1,0:T(8,128)(2,1)}, u32[]{:S(2)}, u32[]{:S(2)}) %all-to-all-start.1) | async-done | bytes 4259872 | tf_op jit(solution)/shard_map/all_to_all | solution.py:292
  149.1 0.9 convert_reduce_fusion
  150.0 0.1 slice.23
  150.1 3.1 %collective-permute-start.14 = (f32[8,48]{1,0:T(8,128)S(1)}, f32[8,48]{1,0:T(8,128)S(1)}, u32[]{:S(2)}, u32[]{:S(2)}) collective-permute-start(f32[8,48]{1,0:T(8,128)S(1)} %slice.23), channel_id=1, source_target_pairs={{255,0},{0,1},{1,2},{2,3},{3,4},{4,5},{5,6},{6,7},{7,8},{8,9},{9,1... | collective-permute-start | bytes 4616 | tf_op jit(solution)/shard_map/ppermute | solution.py:298
  153.2 0.0 collective-permute-done.13
  153.2 0.0 collective-permute-done.10
  153.2 0.1 add_bitcast_fusion
  153.3 1.4 copy.12
  154.7 8.2 %unpack.1 = (bf16[1024,512]{1,0:T(8,128)(2,1)}, bf16[1024,512]{1,0:T(8,128)(2,1)}) custom-call(s32[8,1024]{1,0:T(8,128)} %get-tuple-element.20.pos_ref, bf16[32,520,128]{2,1,0:T(8,128)(2,1)} %all-to-all-done.1.back_ref), custom_call_target="tpu_custom_call" | custom-call | tf_op jit(solution)/shard_map/unpack/pallas_call | solution.py:277
  162.8 0.0 collective-permute-done.14
  162.8 0.6 slice_add_fusion
  (13 shorter events, 0.0 us)
Async XLA Ops:
  9.6 7.6 %copy-start.8 = (bf16[1,262,512]{2,1,0:T(8,128)(2,1)S(1)}, bf16[1,262,512]{2,1,0:T(8,128)(2,1)}, u32[]{:S(2)}) copy-start(bf16[1,262,512]{2,1,0:T(8,128)(2,1)} %param.11) | copy-start | bytes 804868
  9.6 38.0 %copy-start.10 = (bf16[2048,48]{0,1:T(8,128)(2,1)S(1)}, bf16[2048,48]{0,1:T(8,128)(2,1)}, u32[]{:S(2)}) copy-start(bf16[2048,48]{0,1:T(8,128)(2,1)} %param.10) | copy-start | bytes 589828
  9.6 38.0 %slice-start = ((bf16[2048,48]{0,1:T(8,128)(2,1)}), bf16[64,48]{0,1:T(8,128)(2,1)S(1)}, s32[]{:S(2)}) async-start(bf16[2048,48]{0,1:T(8,128)(2,1)} %param.10), calls=%async_computation.2 | async-start | bytes 24576 | tf_op jit(solution)/shard_map/slice | solution.py:338
  9.6 61.9 %all-to-all-start = ((bf16[32,520,128]{2,1,0:T(8,128)(2,1)}), bf16[32,520,128]{2,1,0:T(8,128)(2,1)}, u32[]{:S(2)}, u32[]{:S(2)}) async-start(bf16[32,520,128]{2,1,0:T(8,128)(2,1)} %get-tuple-element.21), calls=%async_computation | async-start | bytes 8519680 | tf_op jit(solution)/shard_map/all_to_all | solution.py:292
  17.2 34.4 %copy-start = (bf16[264,512]{1,0:T(8,128)(2,1)}, bf16[264,512]{1,0:T(8,128)(2,1)S(1)}, u32[]{:S(2)}) copy-start(bf16[264,512]{1,0:T(8,128)(2,1)S(1)} %pad.4.refs_0_) | copy-start | bytes 811012
  17.2 9.3 %collective-permute-start = (bf16[264,512]{1,0:T(8,128)(2,1)S(1)}, bf16[264,512]{1,0:T(8,128)(2,1)S(1)}, u32[]{:S(2)}, u32[]{:S(2)}) collective-permute-start(bf16[264,512]{1,0:T(8,128)(2,1)S(1)} %pad.4.refs_0_), channel_id=1, source_target_pairs={{7,0},{0,1},{1,2},{2,3},{3,4},{4,5},{5,6},{6,7},{15,8},{8,9},{9,10... | collective-permute-start | bytes 811016 | tf_op jit(solution)/shard_map/ppermute | solution.py:298
  20.4 9.8 %collective-permute-start.1 = (bf16[264,512]{1,0:T(8,128)(2,1)S(1)}, bf16[264,512]{1,0:T(8,128)(2,1)S(1)}, u32[]{:S(2)}, u32[]{:S(2)}) collective-permute-start(bf16[264,512]{1,0:T(8,128)(2,1)S(1)} %pad.4.refs_0_), channel_id=1, source_target_pairs={{1,0},{2,1},{3,2},{4,3},{5,4},{6,5},{7,6},{0,7},{9,8},{10,9},{11,1... | collective-permute-start | bytes 811016 | tf_op jit(solution)/shard_map/ppermute | solution.py:298
  26.5 25.1 %copy-start.1 = (bf16[264,512]{1,0:T(8,128)(2,1)}, bf16[264,512]{1,0:T(8,128)(2,1)S(1)}, u32[]{:S(2)}) copy-start(bf16[264,512]{1,0:T(8,128)(2,1)S(1)} %collective-permute-done.refs_1_) | copy-start | bytes 811012
  26.5 9.1 %collective-permute-start.2 = (bf16[264,512]{1,0:T(8,128)(2,1)S(1)}, bf16[264,512]{1,0:T(8,128)(2,1)S(1)}, u32[]{:S(2)}, u32[]{:S(2)}) collective-permute-start(bf16[264,512]{1,0:T(8,128)(2,1)S(1)} %collective-permute-done.refs_1_), channel_id=1, source_target_pairs={{7,0},{0,1},{1,2},{2,3},{3,4},{4,5},{5,6},{6,7},{15,8},{8,9},{9,10... | collective-permute-start | bytes 811016 | tf_op jit(solution)/shard_map/ppermute | solution.py:298
  30.2 21.4 %copy-start.2 = (bf16[264,512]{1,0:T(8,128)(2,1)}, bf16[264,512]{1,0:T(8,128)(2,1)S(1)}, u32[]{:S(2)}) copy-start(bf16[264,512]{1,0:T(8,128)(2,1)S(1)} %collective-permute-done.1.refs_2_) | copy-start | bytes 811012
  30.2 9.1 %collective-permute-start.3 = (bf16[264,512]{1,0:T(8,128)(2,1)S(1)}, bf16[264,512]{1,0:T(8,128)(2,1)S(1)}, u32[]{:S(2)}, u32[]{:S(2)}) collective-permute-start(bf16[264,512]{1,0:T(8,128)(2,1)S(1)} %collective-permute-done.1.refs_2_), channel_id=1, source_target_pairs={{1,0},{2,1},{3,2},{4,3},{5,4},{6,5},{7,6},{0,7},{9,8},{10,9},{11,1... | collective-permute-start | bytes 811016 | tf_op jit(solution)/shard_map/ppermute | solution.py:298
  35.6 16.0 %copy-start.3 = (bf16[264,512]{1,0:T(8,128)(2,1)}, bf16[264,512]{1,0:T(8,128)(2,1)S(1)}, u32[]{:S(2)}) copy-start(bf16[264,512]{1,0:T(8,128)(2,1)S(1)} %collective-permute-done.2.refs_3_) | copy-start | bytes 811012
  35.6 8.3 %collective-permute-start.4 = (bf16[264,512]{1,0:T(8,128)(2,1)S(1)}, bf16[264,512]{1,0:T(8,128)(2,1)S(1)}, u32[]{:S(2)}, u32[]{:S(2)}) collective-permute-start(bf16[264,512]{1,0:T(8,128)(2,1)S(1)} %collective-permute-done.2.refs_3_), channel_id=1, source_target_pairs={{7,0},{0,1},{1,2},{2,3},{3,4},{4,5},{5,6},{6,7},{15,8},{8,9},{9,10... | collective-permute-start | bytes 811016 | tf_op jit(solution)/shard_map/ppermute | solution.py:298
  39.3 12.3 %copy-start.4 = (bf16[264,512]{1,0:T(8,128)(2,1)}, bf16[264,512]{1,0:T(8,128)(2,1)S(1)}, u32[]{:S(2)}) copy-start(bf16[264,512]{1,0:T(8,128)(2,1)S(1)} %collective-permute-done.3.refs_4_) | copy-start | bytes 811012
  39.3 9.9 %collective-permute-start.5 = (bf16[264,512]{1,0:T(8,128)(2,1)S(1)}, bf16[264,512]{1,0:T(8,128)(2,1)S(1)}, u32[]{:S(2)}, u32[]{:S(2)}) collective-permute-start(bf16[264,512]{1,0:T(8,128)(2,1)S(1)} %collective-permute-done.3.refs_4_), channel_id=1, source_target_pairs={{1,0},{2,1},{3,2},{4,3},{5,4},{6,5},{7,6},{0,7},{9,8},{10,9},{11,1... | collective-permute-start | bytes 811016 | tf_op jit(solution)/shard_map/ppermute | solution.py:298
  43.9 7.7 %copy-start.5 = (bf16[264,512]{1,0:T(8,128)(2,1)}, bf16[264,512]{1,0:T(8,128)(2,1)S(1)}, u32[]{:S(2)}) copy-start(bf16[264,512]{1,0:T(8,128)(2,1)S(1)} %collective-permute-done.4.refs_5_) | copy-start | bytes 811012
  43.9 7.7 %collective-permute-start.6 = (bf16[264,512]{1,0:T(8,128)(2,1)S(1)}, bf16[264,512]{1,0:T(8,128)(2,1)S(1)}, u32[]{:S(2)}, u32[]{:S(2)}) collective-permute-start(bf16[264,512]{1,0:T(8,128)(2,1)S(1)} %collective-permute-done.4.refs_5_), channel_id=1, source_target_pairs={{7,0},{0,1},{1,2},{2,3},{3,4},{4,5},{5,6},{6,7},{15,8},{8,9},{9,10... | collective-permute-start | bytes 811016 | tf_op jit(solution)/shard_map/ppermute | solution.py:298
  49.3 2.4 %copy-start.6 = (bf16[264,512]{1,0:T(8,128)(2,1)}, bf16[264,512]{1,0:T(8,128)(2,1)S(1)}, u32[]{:S(2)}) copy-start(bf16[264,512]{1,0:T(8,128)(2,1)S(1)} %collective-permute-done.5.refs_6_) | copy-start | bytes 811012
  51.6 0.7 copy-start.7
  89.8 59.4 %all-to-all-start.1 = ((bf16[32,520,128]{2,1,0:T(8,128)(2,1)}), bf16[32,520,128]{2,1,0:T(8,128)(2,1)}, u32[]{:S(2)}, u32[]{:S(2)}) async-start(bf16[32,520,128]{2,1,0:T(8,128)(2,1)} %get-tuple-element.22), calls=%async_computation.1 | async-start | bytes 8519680 | tf_op jit(solution)/shard_map/all_to_all | solution.py:292
  105.7 47.5 %copy-start.9 = (bf16[264,512]{1,0:T(8,128)(2,1)S(1)}, bf16[264,512]{1,0:T(8,128)(2,1)}, u32[]{:S(2)}) copy-start(bf16[264,512]{1,0:T(8,128)(2,1)} %get-tuple-element.35) | copy-start | bytes 811012
  105.7 9.5 %collective-permute-start.7 = (bf16[264,512]{1,0:T(8,128)(2,1)}, bf16[264,512]{1,0:T(8,128)(2,1)S(1)}, u32[]{:S(2)}, u32[]{:S(2)}) collective-permute-start(bf16[264,512]{1,0:T(8,128)(2,1)} %get-tuple-element.28), channel_id=1, source_target_pairs={{7,0},{0,1},{1,2},{2,3},{3,4},{4,5},{5,6},{6,7},{15,8},{8,9},{9,10... | collective-permute-start | bytes 811016 | tf_op jit(solution)/shard_map/ppermute | solution.py:298
  108.9 11.0 %collective-permute-start.11 = (bf16[264,512]{1,0:T(8,128)(2,1)}, bf16[264,512]{1,0:T(8,128)(2,1)S(1)}, u32[]{:S(2)}, u32[]{:S(2)}) collective-permute-start(bf16[264,512]{1,0:T(8,128)(2,1)} %get-tuple-element.32), channel_id=1, source_target_pairs={{1,0},{2,1},{3,2},{4,3},{5,4},{6,5},{7,6},{0,7},{9,8},{10,9},{11,1... | collective-permute-start | bytes 811016 | tf_op jit(solution)/shard_map/ppermute | solution.py:298
  116.2 8.9 %collective-permute-start.8 = (bf16[264,512]{1,0:T(8,128)(2,1)S(1)}, bf16[264,512]{1,0:T(8,128)(2,1)S(1)}, u32[]{:S(2)}, u32[]{:S(2)}) collective-permute-start(bf16[264,512]{1,0:T(8,128)(2,1)S(1)} %add_convert_fusion.4), channel_id=1, source_target_pairs={{7,0},{0,1},{1,2},{2,3},{3,4},{4,5},{5,6},{6,7},{15,8},{8,9},{9,10... | collective-permute-start | bytes 811016 | tf_op jit(solution)/shard_map/ppermute | solution.py:298
  120.9 9.0 %collective-permute-start.12 = (bf16[264,512]{1,0:T(8,128)(2,1)S(1)}, bf16[264,512]{1,0:T(8,128)(2,1)S(1)}, u32[]{:S(2)}, u32[]{:S(2)}) collective-permute-start(bf16[264,512]{1,0:T(8,128)(2,1)S(1)} %add_convert_fusion.1), channel_id=1, source_target_pairs={{1,0},{2,1},{3,2},{4,3},{5,4},{6,5},{7,6},{0,7},{9,8},{10,9},{11,1... | collective-permute-start | bytes 811016 | tf_op jit(solution)/shard_map/ppermute | solution.py:298
  126.2 8.2 %collective-permute-start.9 = (bf16[264,512]{1,0:T(8,128)(2,1)S(1)}, bf16[264,512]{1,0:T(8,128)(2,1)S(1)}, u32[]{:S(2)}, u32[]{:S(2)}) collective-permute-start(bf16[264,512]{1,0:T(8,128)(2,1)S(1)} %add_convert_fusion.3), channel_id=1, source_target_pairs={{7,0},{0,1},{1,2},{2,3},{3,4},{4,5},{5,6},{6,7},{15,8},{8,9},{9,10... | collective-permute-start | bytes 811016 | tf_op jit(solution)/shard_map/ppermute | solution.py:298
  131.0 22.2 %collective-permute-start.13 = (bf16[264,512]{1,0:T(8,128)(2,1)S(1)}, bf16[264,512]{1,0:T(8,128)(2,1)S(1)}, u32[]{:S(2)}, u32[]{:S(2)}) collective-permute-start(bf16[264,512]{1,0:T(8,128)(2,1)S(1)} %add_convert_fusion), channel_id=1, source_target_pairs={{1,0},{2,1},{3,2},{4,3},{5,4},{6,5},{7,6},{0,7},{9,8},{10,9},{11,1... | collective-permute-start | bytes 811016 | tf_op jit(solution)/shard_map/ppermute | solution.py:298
  135.4 17.8 %collective-permute-start.10 = (bf16[264,512]{1,0:T(8,128)(2,1)S(1)}, bf16[264,512]{1,0:T(8,128)(2,1)S(1)}, u32[]{:S(2)}, u32[]{:S(2)}) collective-permute-start(bf16[264,512]{1,0:T(8,128)(2,1)S(1)} %add_convert_fusion.2), channel_id=1, source_target_pairs={{7,0},{0,1},{1,2},{2,3},{3,4},{4,5},{5,6},{6,7},{15,8},{8,9},{9,10... | collective-permute-start | bytes 811016 | tf_op jit(solution)/shard_map/ppermute | solution.py:298
  150.1 12.8 %collective-permute-start.14 = (f32[8,48]{1,0:T(8,128)S(1)}, f32[8,48]{1,0:T(8,128)S(1)}, u32[]{:S(2)}, u32[]{:S(2)}) collective-permute-start(f32[8,48]{1,0:T(8,128)S(1)} %slice.23), channel_id=1, source_target_pairs={{255,0},{0,1},{1,2},{2,3},{3,4},{4,5},{5,6},{6,7},{7,8},{8,9},{9,1... | collective-permute-start | bytes 4616 | tf_op jit(solution)/shard_map/ppermute | solution.py:298

commit v2 on v1

v2 whole, which is shorter than its diff:
```python
import jax
import jax.numpy as jnp
from jax import lax
from jax.experimental import pallas as pl
from jax.experimental.pallas import tpu as pltpu
from jax.sharding import PartitionSpec as P

LAYERS = 4
D = 512
CODE = 48
ROWS_DEV = 1024
IMG_DEV = 8
CAP = 64
PEERS = 32
NARROW = 8
LANES = 128
CHUNKS = D // LANES
TAIL = 8
BLOCK = 2 * CHUNKS * CAP + TAIL
SHARD = 262
SHARD_PAD = 264
PROWS = 2096
F32 = jnp.float32
BF16 = jnp.bfloat16
MIB = 1024 * 1024


def params_of(mib):
    return pltpu.CompilerParams(vmem_limit_bytes=mib * MIB)


def cost(us):
    return pl.CostEstimate(flops=0, transcendentals=0, bytes_accessed=us * 3_000_000)


def in_vmem():
    return pl.BlockSpec(memory_space=pltpu.VMEM)


def in_smem():
    return pl.BlockSpec(memory_space=pltpu.SMEM)


def in_hbm():
    return pl.BlockSpec(memory_space=pltpu.HBM)


def pinned(*values):
    return [pltpu.with_memory_space_constraint(v, pltpu.HBM) for v in values]


def dot(a, b, ca=1, cb=0):
    return lax.dot_general(a, b, (((ca,), (cb,)), ((), ())), preferred_element_type=F32)


SLOTS = PEERS * CAP
PACK_PEERS = 4


def column_of(half, c):
    r = (half * CHUNKS + c) * CAP
    return slice(r, r + CAP)


def pack_body(
    first_ref, routes_hbm, ids_hbm, feats_hbm, cot_hbm, out_hbm, pos_ref, routes_ref, ids_ref, feats_ref, cot_ref, out_ref, sems
):
    sources = (feats_ref, cot_ref)
    small, loads = [
        [pltpu.make_async_copy(hbm, ref, sems.at[i]) for i, hbm, ref in group]
        for group in (
            ((0, routes_hbm, routes_ref), (1, ids_hbm, ids_ref)),
            ((2, feats_hbm, feats_ref), (3, cot_hbm, cot_ref)),
        )
    ]
    for load in small + loads:
        load.start()
    for load in small:
        load.wait()
    width = 256
    upper = (
        lax.broadcasted_iota(jnp.int32, (width, width), 0)
        <= lax.broadcasted_iota(jnp.int32, (width, width), 1)
    ).astype(F32).astype(BF16)
    expert = lax.broadcasted_iota(jnp.int32, (PEERS, width), 0)
    base = (expert * CAP - 1).astype(F32)
    carry = jnp.zeros((PEERS, 1), F32)
    tail = jnp.zeros((PEERS, CAP), F32)
    off = ids_ref[...] - first_ref[0]
    off = (jnp.where(off < 0, off + PEERS * NARROW * IMG_DEV, off) + 1).astype(F32)
    for b in range(ROWS_DEV // width):
        part = slice(b * width, (b + 1) * width)
        hot = (routes_ref[:, part] == expert).astype(F32)
        rank = dot(hot.astype(BF16), upper) + carry
        carry = carry + jnp.sum(hot, axis=1, keepdims=True)
        pos_ref[:, part] = jnp.sum(hot * (rank + base), axis=0, keepdims=True).astype(jnp.int32)
        slot = jnp.sum(hot * rank, axis=0, keepdims=True).astype(jnp.int32) - 1
        at = (lax.broadcasted_iota(jnp.int32, (CAP, width), 0) == slot).astype(F32).astype(BF16)
        tail = tail + dot((hot * off[:, part]).astype(BF16), at, 1, 1)
    tail = jnp.concatenate([tail, jnp.zeros((PEERS, LANES - CAP), F32)], axis=1)
    n = PACK_PEERS * CAP
    stores = []
    for g in range(PEERS // PACK_PEERS):
        peers = slice(g * PACK_PEERS, (g + 1) * PACK_PEERS)
        slot = lax.broadcasted_iota(jnp.int32, (n, ROWS_DEV), 0) + g * n
        pick = (pos_ref[...] == slot).astype(F32).astype(BF16)
        for half, src in enumerate(sources):
            if g == 0:
                loads[half].wait()
            got = dot(pick, src[...]).astype(BF16)
            for c in range(CHUNKS):
                out_ref[peers, column_of(half, c), :] = got[:, c * LANES : (c + 1) * LANES].reshape(
                    PACK_PEERS, CAP, LANES
                )
        for e in range(g * PACK_PEERS, (g + 1) * PACK_PEERS):
            out_ref[e, BLOCK - TAIL :, :] = jnp.broadcast_to(tail[e : e + 1], (TAIL, LANES)).astype(BF16)
        stores.append(pltpu.make_async_copy(out_ref.at[peers], out_hbm.at[peers], sems.at[4 + g]))
        stores[-1].start()
    for store in stores:
        store.wait()


def pack(first, routes, ids, feats, cot):
    return pl.pallas_call(
        pack_body,
        in_specs=[in_smem()] + [in_hbm()] * 4,
        out_specs=[in_hbm(), in_vmem()],
        scratch_shapes=[
            pltpu.VMEM((1, ROWS_DEV), jnp.int32),
            pltpu.VMEM((1, ROWS_DEV), jnp.int32),
            pltpu.VMEM((ROWS_DEV, D), BF16),
            pltpu.VMEM((ROWS_DEV, D), BF16),
            pltpu.VMEM((PEERS, BLOCK, LANES), BF16),
            pltpu.SemaphoreType.DMA((4 + PEERS // PACK_PEERS,)),
        ],
        out_shape=[
            pltpu.HBM((PEERS, BLOCK, LANES), BF16),
            jax.ShapeDtypeStruct((1, ROWS_DEV), jnp.int32),
        ],
        compiler_params=params_of(32),
        cost_estimate=cost(8),
        name="pack",
    )(first, *pinned(routes, ids, feats, cot))


HOPS = (0, -1, 1, -2, 2, -3, 3, -4)


def join_body(narrow_ref, *refs):
    shard_refs, (out_ref, order, scr) = refs[:NARROW], refs[NARROW:]
    for hop, ref in zip(HOPS, shard_refs):
        order[(narrow_ref[0] + hop + NARROW) % NARROW] = ref[...]
    for n in range(NARROW):
        scr[n * SHARD : (n + 1) * SHARD, :] = order[n, :SHARD, :].astype(F32)
    out_ref[...] = scr[...].astype(BF16)


def join(narrow, shards):
    return pl.pallas_call(
        join_body,
        in_specs=[in_smem()] + [in_vmem()] * NARROW,
        out_specs=in_vmem(),
        scratch_shapes=[pltpu.VMEM((NARROW, SHARD_PAD, D), BF16), pltpu.VMEM((PROWS, D), F32)],
        out_shape=jax.ShapeDtypeStruct((PROWS, D), BF16),
        compiler_params=params_of(12),
        cost_estimate=cost(4),
        name="join",
    )(narrow, *shards)


EXP_PEERS = 16
EXP_ROWS = EXP_PEERS * CAP
EXP_STEPS = PEERS // EXP_PEERS
WIN = 2 * IMG_DEV


def expert_body(
    got_hbm, win_ref, w_ref, out_hbm, z_hbm, err_hbm, code_ref, got_ref, out_ref, z_ref, err_ref, loads, stores, z_sems, err_sems
):
    weights = lambda l: w_ref[l * D : (l + 1) * D, :]
    code_matrix = w_ref[LAYERS * D :, :]
    all_peers = [slice(k * EXP_PEERS, (k + 1) * EXP_PEERS) for k in range(EXP_STEPS)]
    inputs = [pltpu.make_async_copy(got_hbm.at[p], got_ref.at[p], loads.at[k]) for k, p in enumerate(all_peers)]
    for load in inputs:
        load.start()
    outputs = []
    pending = {}
    for k, peers in enumerate(all_peers):
        span = slice(k * EXP_ROWS, (k + 1) * EXP_ROWS)
        buf = k % 2

        def save(kind, ref, hbm, sems, l, value):
            if (kind, buf, l) in pending:
                pending[kind, buf, l].wait()
            ref[buf, l] = value
            pending[kind, buf, l] = pltpu.make_async_copy(ref.at[buf, l], hbm.at[l, span], sems.at[buf, l])
            pending[kind, buf, l].start()

        def columns(half):
            parts = [got_ref[peers, column_of(half, c), :].reshape(EXP_ROWS, LANES) for c in range(CHUNKS)]
            return jnp.concatenate(parts, axis=1)

        def store_columns(half, value):
            for c in range(CHUNKS):
                out_ref[peers, column_of(half, c), :] = value[:, c * LANES : (c + 1) * LANES].reshape(
                    EXP_PEERS, CAP, LANES
                )

        inputs[k].wait()
        image = lax.broadcasted_iota(jnp.int32, (EXP_PEERS * WIN, EXP_ROWS), 0) + 1
        key = jnp.concatenate(
            [
                jnp.where(v > 0.0, v + float(j * WIN), 0.0)
                for j in range(EXP_PEERS)
                for v in [got_ref[k * EXP_PEERS + j, BLOCK - TAIL :, :CAP].astype(F32)]
            ],
            axis=1,
        )[0:1]
        hot = (key.astype(jnp.int32) == image).astype(F32).astype(BF16)
        window = win_ref[k * EXP_PEERS * WIN : (k + 1) * EXP_PEERS * WIN, :]
        code_rows = dot(hot, window, 0, 0).astype(BF16)
        code_ref[span, :] = code_rows
        current = columns(0)
        slopes = []
        for l in range(LAYERS):
            save("z", z_ref, z_hbm, z_sems, l, current)
            pre = dot(current, weights(l))
            if l == 0:
                pre = pre + dot(code_rows, code_matrix)
            s = 0.5 * jnp.tanh(0.5 * pre) + 0.5
            act = pre * s
            slopes.append(s + act * (1.0 - s))
            current = act.astype(BF16)
        store_columns(0, current)
        up = columns(1).astype(F32)
        for l in range(LAYERS - 1, -1, -1):
            err = (up * slopes[l]).astype(BF16)
            save("err", err_ref, err_hbm, err_sems, l, err)
            up = dot(err, weights(l), 1, 1)
        code_back = dot(err, code_matrix, 1, 1).astype(BF16)
        store_columns(1, up.astype(BF16))
        sums = dot(hot, code_back)
        pad = jnp.zeros((IMG_DEV, LANES // 2 - CODE), F32)
        for j in range(EXP_PEERS):
            low = sums[j * WIN : j * WIN + IMG_DEV]
            high = sums[j * WIN + IMG_DEV : (j + 1) * WIN]
            out_ref[k * EXP_PEERS + j, BLOCK - TAIL :, :] = jnp.concatenate([low, pad, high, pad], axis=1).astype(BF16)
        outputs.append(pltpu.make_async_copy(out_ref.at[peers], out_hbm.at[peers], stores.at[k]))
        outputs[-1].start()
    for store in list(pending.values()) + outputs:
        store.wait()


def expert(got, window, weights):
    return pl.pallas_call(
        expert_body,
        in_specs=[in_hbm(), in_vmem(), in_vmem()],
        out_specs=[in_hbm(), in_hbm(), in_hbm(), in_vmem()],
        scratch_shapes=[
            pltpu.VMEM((PEERS, BLOCK, LANES), BF16),
            pltpu.VMEM((PEERS, BLOCK, LANES), BF16),
            pltpu.VMEM((2, LAYERS, EXP_ROWS, D), BF16),
            pltpu.VMEM((2, LAYERS, EXP_ROWS, D), BF16),
            pltpu.SemaphoreType.DMA((EXP_STEPS,)),
            pltpu.SemaphoreType.DMA((EXP_STEPS,)),
            pltpu.SemaphoreType.DMA((2, LAYERS)),
            pltpu.SemaphoreType.DMA((2, LAYERS)),
        ],
        out_shape=[
            pltpu.HBM((PEERS, BLOCK, LANES), BF16),
            pltpu.HBM((LAYERS, SLOTS, D), BF16),
            pltpu.HBM((LAYERS, SLOTS, D), BF16),
            jax.ShapeDtypeStruct((SLOTS, CODE), BF16),
        ],
        compiler_params=params_of(44),
        cost_estimate=cost(17),
        name="expert",
    )(*pinned(got), window, weights)


def grads_body(narrow_ref, z_ref, err_ref, code_ref, *refs):
    out_refs, (scr, order) = refs[:NARROW], refs[NARROW:]
    l = pl.program_id(0)
    scr[pl.ds(pl.multiple_of(l * D, D), D), :] = dot(z_ref[0], err_ref[0], 0, 0)

    @pl.when(l == 0)
    def _():
        scr[LAYERS * D :, :] = dot(code_ref[...], err_ref[0], 0, 0)

    @pl.when(l == LAYERS - 1)
    def _():
        for n in range(NARROW):
            order[n, :SHARD, :] = scr[n * SHARD : (n + 1) * SHARD, :].astype(BF16)
            order[n, SHARD:, :] = jnp.zeros((SHARD_PAD - SHARD, D), BF16)
        for k, ref in enumerate(out_refs):
            ref[...] = order[(narrow_ref[0] + k) % NARROW]


def grads(narrow, z, err, code):
    rows = PEERS * CAP
    return pl.pallas_call(
        grads_body,
        grid_spec=pltpu.PrefetchScalarGridSpec(
            num_scalar_prefetch=1,
            grid=(LAYERS,),
            in_specs=[
                pl.BlockSpec((1, rows, D), lambda i, n: (i, 0, 0)),
                pl.BlockSpec((1, rows, D), lambda i, n: (i, 0, 0)),
                pl.BlockSpec((rows, CODE), lambda i, n: (0, 0)),
            ],
            out_specs=[pl.BlockSpec((SHARD_PAD, D), lambda i, n: (0, 0))] * NARROW,
            scratch_shapes=[pltpu.VMEM((PROWS, D), F32), pltpu.VMEM((NARROW, SHARD_PAD, D), BF16)],
        ),
        out_shape=[jax.ShapeDtypeStruct((SHARD_PAD, D), BF16)] * NARROW,
        compiler_params=params_of(40),
        cost_estimate=cost(10),
        name="grads",
    )(narrow, z, err, code)


TILE = 8
UNROLL = 32
UNPACK_PEERS = 4
UNPACK_ROWS = 256


def unpack_body(pos_ref, back_hbm, out_hbm, feat_hbm, back_ref, slots, rows, out_ref, feat_ref, loads, sems):
    all_peers = [slice(k, k + UNPACK_PEERS) for k in range(0, PEERS, UNPACK_PEERS)]
    inputs = [pltpu.make_async_copy(back_hbm.at[p], back_ref.at[p], loads.at[k]) for k, p in enumerate(all_peers)]
    for load in inputs:
        load.start()
    n = UNPACK_PEERS * CAP
    for k, peers in enumerate(all_peers):
        inputs[k].wait()
        for half in range(2):
            for c in range(CHUNKS):
                got = back_ref[peers, column_of(half, c), :].reshape(n, LANES).astype(F32)
                slots[pl.ds(k * n * TILE + half * CHUNKS + c, n, stride=TILE), :] = got
    stores = []
    for part in range(ROWS_DEV // UNPACK_ROWS):
        span = slice(part * UNPACK_ROWS, (part + 1) * UNPACK_ROWS)

        def move(i, _):
            for u in range(UNROLL):
                r = part * UNPACK_ROWS + i * UNROLL + u
                p = pos_ref[0, r]
                rows[pl.ds(pl.multiple_of(r * TILE, TILE), TILE), :] = slots[
                    pl.ds(pl.multiple_of(p * TILE, TILE), TILE), :
                ]
            return 0

        lax.fori_loop(0, UNPACK_ROWS // UNROLL, move, 0)
        for half, (dst, hbm) in enumerate(((out_ref, out_hbm), (feat_ref, feat_hbm))):
            for c in range(CHUNKS):
                dst[span, c * LANES : (c + 1) * LANES] = rows[
                    pl.ds(part * UNPACK_ROWS * TILE + half * CHUNKS + c, UNPACK_ROWS, stride=TILE), :
                ].astype(BF16)
            store = pltpu.make_async_copy(dst.at[span], hbm.at[span], sems.at[part, half])
            store.start()
            stores.append(store)
    for store in stores:
        store.wait()


def unpack(pos, back):
    return pl.pallas_call(
        unpack_body,
        in_specs=[in_smem(), in_hbm()],
        out_specs=[in_hbm()] * 2,
        scratch_shapes=[
            pltpu.VMEM((PEERS, BLOCK, LANES), BF16),
            pltpu.VMEM((SLOTS * TILE, LANES), F32),
            pltpu.VMEM((ROWS_DEV * TILE, LANES), F32),
            pltpu.VMEM((ROWS_DEV, D), BF16),
            pltpu.VMEM((ROWS_DEV, D), BF16),
            pltpu.SemaphoreType.DMA((PEERS // UNPACK_PEERS,)),
            pltpu.SemaphoreType.DMA((ROWS_DEV // UNPACK_ROWS, 2)),
        ],
        out_shape=[pltpu.HBM((ROWS_DEV, D), BF16)] * 2,
        compiler_params=params_of(32),
        cost_estimate=cost(7),
        name="unpack",
    )(pos, *pinned(back))


def exchange(values):
    return lax.all_to_all(values, "expert", split_axis=0, concat_axis=0, tiled=True)


def shifted(block, axis, distance):
    devices = range(lax.axis_size(axis))
    route = [((i - distance) % len(devices), i) for i in devices]
    return lax.ppermute(block, axis, route)


def ring_gather(own):
    got = [own]
    ahead = behind = own
    for step in range(1, NARROW // 2 + 1):
        ahead = shifted(ahead, "narrow", 1)
        got.append(ahead)
        if step < NARROW // 2:
            behind = shifted(behind, "narrow", -1)
            got.append(behind)
    return got


def ring_reduce(terms):
    add = lambda a, b: a.astype(F32) + b.astype(F32)
    half = NARROW // 2
    ahead, behind = terms[half], terms[half + 1]
    for step in range(half):
        ahead = shifted(ahead, "narrow", 1)
        if step > 0:
            behind = shifted(behind, "narrow", -1)
        if step < half - 1:
            ahead = add(ahead, terms[half - 1 - step]).astype(BF16)
            if step > 0:
                behind = add(behind, terms[half + 1 + step]).astype(BF16)
    return finish(ahead, behind, terms[0])


def finish_body(a_ref, b_ref, c_ref, out_ref):
    total = a_ref[...].astype(F32) + b_ref[...].astype(F32) + c_ref[...].astype(F32)
    out_ref[:, 0, :] = total[:SHARD]


def finish(a, b, c):
    return pl.pallas_call(
        finish_body,
        in_specs=[in_vmem()] * 3,
        out_specs=in_vmem(),
        out_shape=jax.ShapeDtypeStruct((SHARD, 1, D), F32),
        compiler_params=params_of(8),
        cost_estimate=cost(2),
        name="finish",
    )(a, b, c)


def body(feats, cotangent, routes, image_ids, codes, params):
    flat = lax.axis_index(("expert", "narrow"))
    first_image = (flat * IMG_DEV).astype(jnp.int32).reshape(1)
    narrow = lax.axis_index("narrow").astype(jnp.int32)
    packed, pos = pack(
        first_image, routes.reshape(1, ROWS_DEV), image_ids.reshape(1, ROWS_DEV), feats, cotangent
    )
    got = exchange(packed)
    shards = ring_gather(jnp.pad(params[0], ((0, SHARD_PAD - SHARD), (0, 0))))
    weights = join(narrow.reshape(1), shards)
    ring = jnp.concatenate([codes, codes[:CAP]], axis=0)
    window = lax.dynamic_slice(ring, (narrow * IMG_DEV, 0), (PEERS * CAP, CODE))
    window = window.reshape(PEERS, CAP, CODE)[:, :WIN].reshape(PEERS * WIN, CODE)
    reply, z, err, code_rows = expert(got, window, weights)
    back = exchange(reply)
    mine = ring_reduce(grads(narrow.reshape(1), z, err, code_rows))
    back, mine = lax.optimization_barrier((back, mine))
    param_grad = mine.transpose(1, 0, 2)
    sums = jnp.sum(back[:, BLOCK - TAIL :, :].astype(F32), axis=0)
    high = shifted(sums[:, LANES // 2 : LANES // 2 + CODE], ("expert", "narrow"), 1)
    out_rows, feat_grad = unpack(pos, back)
    return (out_rows, feat_grad, param_grad, sums[:, :CODE] + high)


def solution(mesh):
    rows = P(("expert", "narrow"), None)
    in_specs = (rows, rows, rows, P(("expert", "narrow")), P(), P("expert", "narrow", None))
    out_specs = (rows, rows, P("expert", "narrow", None), rows)
    return jax.shard_map(body, mesh=mesh, in_specs=in_specs, out_specs=out_specs, check_vma=False)
```

time: 164 us -> 158 us (0.963)
  Pallas kernels: 49.9 us -> 40.8 us
  local copies, waits for them, and re-layouts: 3.61 us -> 10.5 us
  other arithmetic: 6.85 us -> 2 us
    unnamed x23 -> x26, local copies, waits for them, and re-layouts: 2.06 us -> 9.57 us
    pallas_call x4 -> x5, Pallas kernels: 39 us -> 32.7 us  [the longest x1 17.3 us: expert(): pl.pallas_call(expert_body, in_specs=[in_hbm(), in_vmem(), in_vmem()], ou...]
    ppermute x15, waiting for transfers between devices: 32.2 us -> 37.7 us  [shifted(): return lax.ppermute(block, axis, route)]
    all_to_all x2, waiting for transfers between devices: 25.4 us -> 21 us  [exchange(): lax.all_to_all(values, 'expert', split_axis=0, concat_axis=0, tiled=True)]
    convert_element_type x3, other arithmetic: 3.06 us -> 0.21 us  [ring_reduce(): ahead = add(ahead, terms[half - 1 - step]).astype(BF16)]
    pallas_call x1, Pallas kernels: 10.9 us -> 8.14 us  [grads(): pl.pallas_call(grads_body, grid_spec=pltpu.PrefetchScalarGridSpec(num_sca...]
    convert_element_type x2, other arithmetic: 2.04 us -> 0.14 us  [ring_reduce(): behind = add(behind, terms[half + 1 + step]).astype(BF16)]
  transfers between devices with their start and end apart: 17 -> 17, of which waited for: 9 -> 10; matrix products, arithmetic and copies ran while one was open for 6% -> 1% of each run, Pallas kernels for 14% -> 11%
where the time goes in v2:
time: 158 us
  waiting for transfers between devices  58.7 us (37%)
  starting transfers between devices  44.8 us (28%)
  Pallas kernels  40.8 us (26%)
  local copies, waits for them, and re-layouts  10.5 us (7%)
  other arithmetic  2 us (1%)
    ppermute x15, waiting for transfers between devices, shifted(): return lax.ppermute(block, axis, route)  37.7 us
    ppermute x15, starting transfers between devices, shifted(): return lax.ppermute(block, axis, route)  32.4 us
    all_to_all x2, waiting for transfers between devices, exchange(): lax.all_to_all(values, 'expert', split_axis=0, concat_axis=0, tiled=True)  21 us
    pallas_call x1, Pallas kernels, expert(): pl.pallas_call(expert_body, in_specs=[in_hbm(), in_vmem(), in_vmem()], ou...  17.3 us
    all_to_all x2, starting transfers between devices, exchange(): lax.all_to_all(values, 'expert', split_axis=0, concat_axis=0, tiled=True)  12.4 us
    unnamed x26, local copies, waits for them, and re-layouts  9.57 us
    pallas_call x1, Pallas kernels, grads(): pl.pallas_call(grads_body, grid_spec=pltpu.PrefetchScalarGridSpec(num_sca...  8.14 us
    pallas_call x1, Pallas kernels, pack(): pl.pallas_call(pack_body, in_specs=[in_smem()] + [in_hbm()] * 4, out_spec...  6.84 us
  transfers between devices with their start and end apart: 17, of which 10 were waited for; matrix products, arithmetic and copies ran while one was open for 1% of the time, Pallas kernels for 11%

profile of v2, /device:TPU:96, one launch (start us, length us, event | category | flops | bytes accessed | tf_op | source)
XLA Modules:
  0.0 157.7 jit_solution(15379385579791660379)
XLA Ops:
  0.6 6.8 %pack.1 = (bf16[32,520,128]{2,1,0:T(8,128)(2,1)}, s32[1,1024]{1,0:T(1,128)S(1)}) custom-call(s32[1]{0:T(128)} %bitcast.first_ref, s32[1,1024]{1,0:T(1,128)} %bitcast.14, s32[1,1024]{1,0:T(1,128)} %bitcast.15, bf16[1024,512]{1,0:T(8,128)(2,1)} %feats_hbm.1, bf16[1024,512]{1,0:T(8,128)(2,1)} %cot_hbm.1), custom_call_target="tpu_custom_call" | custom-call | bytes 24000000 | tf_op jit(solution)/shard_map/pack/pallas_call | solution.py:124
  7.5 0.0 copy-start.11
  7.5 0.0 copy-start.12
  7.5 0.0 slice-start
  7.5 7.6 %all-to-all-start = ((bf16[32,520,128]{2,1,0:T(8,128)(2,1)}), bf16[32,520,128]{2,1,0:T(8,128)(2,1)}, u32[]{:S(2)}, u32[]{:S(2)}) async-start(bf16[32,520,128]{2,1,0:T(8,128)(2,1)} %get-tuple-element.23), calls=%async_computation | async-start | bytes 8519680 | tf_op jit(solution)/shard_map/all_to_all | solution.py:387
  15.1 0.0 copy-done.11
  15.1 3.2 %collective-permute-start = (bf16[264,512]{1,0:T(8,128)(2,1)S(1)}, bf16[264,512]{1,0:T(8,128)(2,1)S(1)}, u32[]{:S(2)}, u32[]{:S(2)}) collective-permute-start(bf16[264,512]{1,0:T(8,128)(2,1)S(1)} %pad.4.refs_0_), channel_id=1, source_target_pairs={{7,0},{0,1},{1,2},{2,3},{3,4},{4,5},{5,6},{6,7},{15,8},{8,9},{9,10... | collective-permute-start | bytes 811016 | tf_op jit(solution)/shard_map/ppermute | solution.py:393
  18.3 0.0 collective-permute-start.1
  18.4 6.1 %collective-permute-done.refs_1_ = bf16[264,512]{1,0:T(8,128)(2,1)S(1)} collective-permute-done((bf16[264,512]{1,0:T(8,128)(2,1)S(1)}, bf16[264,512]{1,0:T(8,128)(2,1)S(1)}, u32[]{:S(2)}, u32[]{:S(2)}) %collective-permute-start) | collective-permute-done | bytes 270368 | tf_op jit(solution)/shard_map/ppermute | solution.py:393
  24.5 3.7 %collective-permute-start.2 = (bf16[264,512]{1,0:T(8,128)(2,1)S(1)}, bf16[264,512]{1,0:T(8,128)(2,1)S(1)}, u32[]{:S(2)}, u32[]{:S(2)}) collective-permute-start(bf16[264,512]{1,0:T(8,128)(2,1)S(1)} %collective-permute-done.refs_1_), channel_id=1, source_target_pairs={{7,0},{0,1},{1,2},{2,3},{3,4},{4,5},{5,6},{6,7},{15,8},{8,9},{9,10... | collective-permute-start | bytes 811016 | tf_op jit(solution)/shard_map/ppermute | solution.py:393
  28.2 0.0 collective-permute-done.1.refs_2_
  28.2 0.0 collective-permute-start.3
  28.2 5.4 %collective-permute-done.2.refs_3_ = bf16[264,512]{1,0:T(8,128)(2,1)S(1)} collective-permute-done((bf16[264,512]{1,0:T(8,128)(2,1)S(1)}, bf16[264,512]{1,0:T(8,128)(2,1)S(1)}, u32[]{:S(2)}, u32[]{:S(2)}) %collective-permute-start.2) | collective-permute-done | bytes 270368 | tf_op jit(solution)/shard_map/ppermute | solution.py:393
  33.6 3.7 %collective-permute-start.4 = (bf16[264,512]{1,0:T(8,128)(2,1)S(1)}, bf16[264,512]{1,0:T(8,128)(2,1)S(1)}, u32[]{:S(2)}, u32[]{:S(2)}) collective-permute-start(bf16[264,512]{1,0:T(8,128)(2,1)S(1)} %collective-permute-done.2.refs_3_), channel_id=1, source_target_pairs={{7,0},{0,1},{1,2},{2,3},{3,4},{4,5},{5,6},{6,7},{15,8},{8,9},{9,10... | collective-permute-start | bytes 811016 | tf_op jit(solution)/shard_map/ppermute | solution.py:393
  37.3 0.0 collective-permute-done.3.refs_4_
  37.3 0.0 collective-permute-start.5
  37.3 4.6 %collective-permute-done.4.refs_5_ = bf16[264,512]{1,0:T(8,128)(2,1)S(1)} collective-permute-done((bf16[264,512]{1,0:T(8,128)(2,1)S(1)}, bf16[264,512]{1,0:T(8,128)(2,1)S(1)}, u32[]{:S(2)}, u32[]{:S(2)}) %collective-permute-start.4) | collective-permute-done | bytes 270368 | tf_op jit(solution)/shard_map/ppermute | solution.py:393
  41.8 3.7 %collective-permute-start.6 = (bf16[264,512]{1,0:T(8,128)(2,1)S(1)}, bf16[264,512]{1,0:T(8,128)(2,1)S(1)}, u32[]{:S(2)}, u32[]{:S(2)}) collective-permute-start(bf16[264,512]{1,0:T(8,128)(2,1)S(1)} %collective-permute-done.4.refs_5_), channel_id=1, source_target_pairs={{7,0},{0,1},{1,2},{2,3},{3,4},{4,5},{5,6},{6,7},{15,8},{8,9},{9,10... | collective-permute-start | bytes 811016 | tf_op jit(solution)/shard_map/ppermute | solution.py:393
  45.5 0.0 copy-done.12
  45.5 0.2 fusion
  45.7 0.4 reshape.30
  46.1 0.5 copy.10
  46.6 0.0 collective-permute-done.5.refs_6_
  46.6 0.7 copy-done.7
  47.3 2.2 %collective-permute-done.6.refs_7_ = bf16[264,512]{1,0:T(8,128)(2,1)S(1)} collective-permute-done((bf16[264,512]{1,0:T(8,128)(2,1)S(1)}, bf16[264,512]{1,0:T(8,128)(2,1)S(1)}, u32[]{:S(2)}, u32[]{:S(2)}) %collective-permute-start.6) | collective-permute-done | bytes 270368 | tf_op jit(solution)/shard_map/ppermute | solution.py:393
  49.5 0.7 copy-done.9
  50.2 1.0 copy-done.2
  51.2 1.0 copy-done.4
  52.1 1.0 copy-done.6
  53.1 1.0 copy-done.8
  54.0 1.0 copy-done.10
  55.0 0.8 join.1.w_ref
  55.8 13.7 %all-to-all-done.got_hbm = bf16[32,520,128]{2,1,0:T(8,128)(2,1)} async-done(((bf16[32,520,128]{2,1,0:T(8,128)(2,1)}), bf16[32,520,128]{2,1,0:T(8,128)(2,1)}, u32[]{:S(2)}, u32[]{:S(2)}) %all-to-all-start) | async-done | bytes 4259872 | tf_op jit(solution)/shard_map/all_to_all | solution.py:387
  69.4 17.3 %expert.1 = (bf16[32,520,128]{2,1,0:T(8,128)(2,1)}, bf16[4,2048,512]{2,1,0:T(8,128)(2,1)}, bf16[4,2048,512]{2,1,0:T(8,128)(2,1)}, bf16[2048,48]{1,0:T(8,128)(2,1)S(1)}) custom-call(bf16[32,520,128]{2,1,0:T(8,128)(2,1)} %all-to-all-done.got_hbm, bf16[512,48]{1,0:T(8,128)(2,1)S(1)} %bitcast.10, bf16[2096,512]{1,0:T(8,128)(2,1)S(1)} %join.1.w_ref), custom_call_target="tpu_custom_call" | custom-call | bytes 51000000 | tf_op jit(solution)/shard_map/expert/pallas_call | solution.py:255
  86.7 4.9 %all-to-all-start.1 = ((bf16[32,520,128]{2,1,0:T(8,128)(2,1)}), bf16[32,520,128]{2,1,0:T(8,128)(2,1)}, u32[]{:S(2)}, u32[]{:S(2)}) async-start(bf16[32,520,128]{2,1,0:T(8,128)(2,1)} %get-tuple-element.24), calls=%async_computation.1 | async-start | bytes 8519680 | tf_op jit(solution)/shard_map/all_to_all | solution.py:387
  91.6 3.4 %copy-done = bf16[4,2048,512]{2,1,0:T(8,128)(2,1)S(1)} copy-done((bf16[4,2048,512]{2,1,0:T(8,128)(2,1)S(1)}, bf16[4,2048,512]{2,1,0:T(8,128)(2,1)}, u32[]{:S(2)}) %copy-start) | copy-done | bytes 8388632
  95.0 8.1 %grads.1 = (bf16[264,512]{1,0:T(8,128)(2,1)S(1)}, bf16[264,512]{1,0:T(8,128)(2,1)S(1)}, bf16[264,512]{1,0:T(8,128)(2,1)S(1)}, bf16[264,512]{1,0:T(8,128)(2,1)S(1...) custom-call(s32[1]{0:T(128)} %bitcast.4.narrow_ref, ...), custom_call_target="tpu_custom_call" | custom-call | bytes 30000000 | tf_op jit(solution)/shard_map/grads/pallas_call | solution.py:301
  103.1 3.2 %collective-permute-start.7 = (bf16[264,512]{1,0:T(8,128)(2,1)S(1)}, bf16[264,512]{1,0:T(8,128)(2,1)S(1)}, u32[]{:S(2)}, u32[]{:S(2)}) collective-permute-start(bf16[264,512]{1,0:T(8,128)(2,1)S(1)} %get-tuple-element.28), channel_id=1, source_target_pairs={{7,0},{0,1},{1,2},{2,3},{3,4},{4,5},{5,6},{6,7},{15,8},{8,9},{9,10... | collective-permute-start | bytes 811016 | tf_op jit(solution)/shard_map/ppermute | solution.py:393
  106.3 0.0 collective-permute-start.11
  106.3 6.0 %collective-permute-done.7 = bf16[264,512]{1,0:T(8,128)(2,1)S(1)} collective-permute-done((bf16[264,512]{1,0:T(8,128)(2,1)S(1)}, bf16[264,512]{1,0:T(8,128)(2,1)S(1)}, u32[]{:S(2)}, u32[]{:S(2)}) %collective-permute-start.7) | collective-permute-done | bytes 270368 | tf_op jit(solution)/shard_map/ppermute | solution.py:393
  112.3 0.1 add_convert_fusion.4
  112.4 3.8 %collective-permute-start.8 = (bf16[264,512]{1,0:T(8,128)(2,1)S(1)}, bf16[264,512]{1,0:T(8,128)(2,1)S(1)}, u32[]{:S(2)}, u32[]{:S(2)}) collective-permute-start(bf16[264,512]{1,0:T(8,128)(2,1)S(1)} %add_convert_fusion.4), channel_id=1, source_target_pairs={{7,0},{0,1},{1,2},{2,3},{3,4},{4,5},{5,6},{6,7},{15,8},{8,9},{9,10... | collective-permute-start | bytes 811016 | tf_op jit(solution)/shard_map/ppermute | solution.py:393
  116.2 0.0 collective-permute-done.11
  116.2 0.1 add_convert_fusion.1
  116.2 0.1 collective-permute-start.12
  116.3 5.1 %collective-permute-done.8 = bf16[264,512]{1,0:T(8,128)(2,1)S(1)} collective-permute-done((bf16[264,512]{1,0:T(8,128)(2,1)S(1)}, bf16[264,512]{1,0:T(8,128)(2,1)S(1)}, u32[]{:S(2)}, u32[]{:S(2)}) %collective-permute-start.8) | collective-permute-done | bytes 270368 | tf_op jit(solution)/shard_map/ppermute | solution.py:393
  121.4 0.1 add_convert_fusion.3
  121.5 3.8 %collective-permute-start.9 = (bf16[264,512]{1,0:T(8,128)(2,1)S(1)}, bf16[264,512]{1,0:T(8,128)(2,1)S(1)}, u32[]{:S(2)}, u32[]{:S(2)}) collective-permute-start(bf16[264,512]{1,0:T(8,128)(2,1)S(1)} %add_convert_fusion.3), channel_id=1, source_target_pairs={{7,0},{0,1},{1,2},{2,3},{3,4},{4,5},{5,6},{6,7},{15,8},{8,9},{9,10... | collective-permute-start | bytes 811016 | tf_op jit(solution)/shard_map/ppermute | solution.py:393
  125.3 0.0 collective-permute-done.12
  125.3 0.1 add_convert_fusion
  125.3 0.1 collective-permute-start.13
  125.4 4.3 %collective-permute-done.9 = bf16[264,512]{1,0:T(8,128)(2,1)S(1)} collective-permute-done((bf16[264,512]{1,0:T(8,128)(2,1)S(1)}, bf16[264,512]{1,0:T(8,128)(2,1)S(1)}, u32[]{:S(2)}, u32[]{:S(2)}) %collective-permute-start.9) | collective-permute-done | bytes 270368 | tf_op jit(solution)/shard_map/ppermute | solution.py:393
  129.7 0.1 add_convert_fusion.2
  129.8 3.8 %collective-permute-start.10 = (bf16[264,512]{1,0:T(8,128)(2,1)S(1)}, bf16[264,512]{1,0:T(8,128)(2,1)S(1)}, u32[]{:S(2)}, u32[]{:S(2)}) collective-permute-start(bf16[264,512]{1,0:T(8,128)(2,1)S(1)} %add_convert_fusion.2), channel_id=1, source_target_pairs={{7,0},{0,1},{1,2},{2,3},{3,4},{4,5},{5,6},{6,7},{15,8},{8,9},{9,10... | collective-permute-start | bytes 811016 | tf_op jit(solution)/shard_map/ppermute | solution.py:393
  133.6 0.0 collective-permute-done.13.b_ref
  133.6 4.0 %collective-permute-done.10.a_ref = bf16[264,512]{1,0:T(8,128)(2,1)S(1)} collective-permute-done((bf16[264,512]{1,0:T(8,128)(2,1)S(1)}, bf16[264,512]{1,0:T(8,128)(2,1)S(1)}, u32[]{:S(2)}, u32[]{:S(2)}) %collective-permute-start.10) | collective-permute-done | bytes 270368 | tf_op jit(solution)/shard_map/ppermute | solution.py:393
  137.5 1.0 finish.1
  138.5 7.4 %all-to-all-done.1.back_hbm = bf16[32,520,128]{2,1,0:T(8,128)(2,1)} async-done(((bf16[32,520,128]{2,1,0:T(8,128)(2,1)}), bf16[32,520,128]{2,1,0:T(8,128)(2,1)}, u32[]{:S(2)}, u32[]{:S(2)}) %all-to-all-start.1) | async-done | bytes 4259872 | tf_op jit(solution)/shard_map/all_to_all | solution.py:387
  145.9 0.9 convert_reduce_fusion
  146.8 0.1 slice.19
  146.9 3.4 %collective-permute-start.14 = (f32[8,48]{1,0:T(8,128)S(1)}, f32[8,48]{1,0:T(8,128)S(1)}, u32[]{:S(2)}, u32[]{:S(2)}) collective-permute-start(f32[8,48]{1,0:T(8,128)S(1)} %slice.19), channel_id=1, source_target_pairs={{255,0},{0,1},{1,2},{2,3},{3,4},{4,5},{5,6},{6,7},{7,8},{8,9},{9,1... | collective-permute-start | bytes 4616 | tf_op jit(solution)/shard_map/ppermute | solution.py:393
  150.2 6.8 %unpack.1 = (bf16[1024,512]{1,0:T(8,128)(2,1)}, bf16[1024,512]{1,0:T(8,128)(2,1)}) custom-call(s32[1,1024]{1,0:T(1,128)S(1)} %get-tuple-element.22.pos_ref, bf16[32,520,128]{2,1,0:T(8,128)(2,1)} %all-to-all-done.1.back_hbm), custom_call_target="tpu_custom_call" | custom-call | bytes 21000000 | tf_op jit(solution)/shard_map/unpack/pallas_call | solution.py:366
  157.1 0.0 collective-permute-done.14
  157.1 0.6 slice_add_fusion
  (16 shorter events, 0.0 us)
Async XLA Ops:
  7.5 7.6 %copy-start.11 = (bf16[1,262,512]{2,1,0:T(8,128)(2,1)S(1)}, bf16[1,262,512]{2,1,0:T(8,128)(2,1)}, u32[]{:S(2)}) copy-start(bf16[1,262,512]{2,1,0:T(8,128)(2,1)} %param.11) | copy-start | bytes 804868
  7.5 38.0 %copy-start.12 = (bf16[2048,48]{0,1:T(8,128)(2,1)S(1)}, bf16[2048,48]{0,1:T(8,128)(2,1)}, u32[]{:S(2)}) copy-start(bf16[2048,48]{0,1:T(8,128)(2,1)} %param.10) | copy-start | bytes 589828
  7.5 38.0 %slice-start = ((bf16[2048,48]{0,1:T(8,128)(2,1)}), bf16[64,48]{0,1:T(8,128)(2,1)S(1)}, s32[]{:S(2)}) async-start(bf16[2048,48]{0,1:T(8,128)(2,1)} %param.10), calls=%async_computation.2 | async-start | bytes 24576 | tf_op jit(solution)/shard_map/slice | solution.py:450
  7.5 61.9 %all-to-all-start = ((bf16[32,520,128]{2,1,0:T(8,128)(2,1)}), bf16[32,520,128]{2,1,0:T(8,128)(2,1)}, u32[]{:S(2)}, u32[]{:S(2)}) async-start(bf16[32,520,128]{2,1,0:T(8,128)(2,1)} %get-tuple-element.23), calls=%async_computation | async-start | bytes 8519680 | tf_op jit(solution)/shard_map/all_to_all | solution.py:387
  15.1 9.3 %collective-permute-start = (bf16[264,512]{1,0:T(8,128)(2,1)S(1)}, bf16[264,512]{1,0:T(8,128)(2,1)S(1)}, u32[]{:S(2)}, u32[]{:S(2)}) collective-permute-start(bf16[264,512]{1,0:T(8,128)(2,1)S(1)} %pad.4.refs_0_), channel_id=1, source_target_pairs={{7,0},{0,1},{1,2},{2,3},{3,4},{4,5},{5,6},{6,7},{15,8},{8,9},{9,10... | collective-permute-start | bytes 811016 | tf_op jit(solution)/shard_map/ppermute | solution.py:393
  18.3 9.8 %collective-permute-start.1 = (bf16[264,512]{1,0:T(8,128)(2,1)S(1)}, bf16[264,512]{1,0:T(8,128)(2,1)S(1)}, u32[]{:S(2)}, u32[]{:S(2)}) collective-permute-start(bf16[264,512]{1,0:T(8,128)(2,1)S(1)} %pad.4.refs_0_), channel_id=1, source_target_pairs={{1,0},{2,1},{3,2},{4,3},{5,4},{6,5},{7,6},{0,7},{9,8},{10,9},{11,1... | collective-permute-start | bytes 811016 | tf_op jit(solution)/shard_map/ppermute | solution.py:393
  24.5 9.1 %collective-permute-start.2 = (bf16[264,512]{1,0:T(8,128)(2,1)S(1)}, bf16[264,512]{1,0:T(8,128)(2,1)S(1)}, u32[]{:S(2)}, u32[]{:S(2)}) collective-permute-start(bf16[264,512]{1,0:T(8,128)(2,1)S(1)} %collective-permute-done.refs_1_), channel_id=1, source_target_pairs={{7,0},{0,1},{1,2},{2,3},{3,4},{4,5},{5,6},{6,7},{15,8},{8,9},{9,10... | collective-permute-start | bytes 811016 | tf_op jit(solution)/shard_map/ppermute | solution.py:393
  28.2 9.1 %collective-permute-start.3 = (bf16[264,512]{1,0:T(8,128)(2,1)S(1)}, bf16[264,512]{1,0:T(8,128)(2,1)S(1)}, u32[]{:S(2)}, u32[]{:S(2)}) collective-permute-start(bf16[264,512]{1,0:T(8,128)(2,1)S(1)} %collective-permute-done.1.refs_2_), channel_id=1, source_target_pairs={{1,0},{2,1},{3,2},{4,3},{5,4},{6,5},{7,6},{0,7},{9,8},{10,9},{11,1... | collective-permute-start | bytes 811016 | tf_op jit(solution)/shard_map/ppermute | solution.py:393
  33.6 12.5 %copy-start.1 = (bf16[264,512]{1,0:T(8,128)(2,1)}, bf16[264,512]{1,0:T(8,128)(2,1)S(1)}, u32[]{:S(2)}) copy-start(bf16[264,512]{1,0:T(8,128)(2,1)S(1)} %collective-permute-done.2.refs_3_) | copy-start | bytes 811012
  33.6 8.3 %collective-permute-start.4 = (bf16[264,512]{1,0:T(8,128)(2,1)S(1)}, bf16[264,512]{1,0:T(8,128)(2,1)S(1)}, u32[]{:S(2)}, u32[]{:S(2)}) collective-permute-start(bf16[264,512]{1,0:T(8,128)(2,1)S(1)} %collective-permute-done.2.refs_3_), channel_id=1, source_target_pairs={{7,0},{0,1},{1,2},{2,3},{3,4},{4,5},{5,6},{6,7},{15,8},{8,9},{9,10... | collective-permute-start | bytes 811016 | tf_op jit(solution)/shard_map/ppermute | solution.py:393
  37.3 12.3 %copy-start.3 = (bf16[264,512]{1,0:T(8,128)(2,1)}, bf16[264,512]{1,0:T(8,128)(2,1)S(1)}, u32[]{:S(2)}) copy-start(bf16[264,512]{1,0:T(8,128)(2,1)S(1)} %collective-permute-done.3.refs_4_) | copy-start | bytes 811012
  37.3 9.3 %collective-permute-start.5 = (bf16[264,512]{1,0:T(8,128)(2,1)S(1)}, bf16[264,512]{1,0:T(8,128)(2,1)S(1)}, u32[]{:S(2)}, u32[]{:S(2)}) collective-permute-start(bf16[264,512]{1,0:T(8,128)(2,1)S(1)} %collective-permute-done.3.refs_4_), channel_id=1, source_target_pairs={{1,0},{2,1},{3,2},{4,3},{5,4},{6,5},{7,6},{0,7},{9,8},{10,9},{11,1... | collective-permute-start | bytes 811016 | tf_op jit(solution)/shard_map/ppermute | solution.py:393
  41.8 7.7 %copy-start.5 = (bf16[264,512]{1,0:T(8,128)(2,1)}, bf16[264,512]{1,0:T(8,128)(2,1)S(1)}, u32[]{:S(2)}) copy-start(bf16[264,512]{1,0:T(8,128)(2,1)S(1)} %collective-permute-done.4.refs_5_) | copy-start | bytes 811012
  41.8 7.7 %collective-permute-start.6 = (bf16[264,512]{1,0:T(8,128)(2,1)S(1)}, bf16[264,512]{1,0:T(8,128)(2,1)S(1)}, u32[]{:S(2)}, u32[]{:S(2)}) collective-permute-start(bf16[264,512]{1,0:T(8,128)(2,1)S(1)} %collective-permute-done.4.refs_5_), channel_id=1, source_target_pairs={{7,0},{0,1},{1,2},{2,3},{3,4},{4,5},{5,6},{6,7},{15,8},{8,9},{9,10... | collective-permute-start | bytes 811016 | tf_op jit(solution)/shard_map/ppermute | solution.py:393
  46.6 0.7 copy-start.7
  49.5 0.7 copy-start.9
  50.2 1.0 copy-start.2
  51.2 1.0 copy-start.4
  52.1 1.0 copy-start.6
  53.1 1.0 copy-start.8
  54.0 1.0 copy-start.10
  86.7 59.2 %all-to-all-start.1 = ((bf16[32,520,128]{2,1,0:T(8,128)(2,1)}), bf16[32,520,128]{2,1,0:T(8,128)(2,1)}, u32[]{:S(2)}, u32[]{:S(2)}) async-start(bf16[32,520,128]{2,1,0:T(8,128)(2,1)} %get-tuple-element.24), calls=%async_computation.1 | async-start | bytes 8519680 | tf_op jit(solution)/shard_map/all_to_all | solution.py:387
  91.6 3.4 %copy-start = (bf16[4,2048,512]{2,1,0:T(8,128)(2,1)S(1)}, bf16[4,2048,512]{2,1,0:T(8,128)(2,1)}, u32[]{:S(2)}) copy-start(bf16[4,2048,512]{2,1,0:T(8,128)(2,1)} %get-tuple-element.25.z_ref) | copy-start | bytes 25165828
  103.1 9.2 %collective-permute-start.7 = (bf16[264,512]{1,0:T(8,128)(2,1)S(1)}, bf16[264,512]{1,0:T(8,128)(2,1)S(1)}, u32[]{:S(2)}, u32[]{:S(2)}) collective-permute-start(bf16[264,512]{1,0:T(8,128)(2,1)S(1)} %get-tuple-element.28), channel_id=1, source_target_pairs={{7,0},{0,1},{1,2},{2,3},{3,4},{4,5},{5,6},{6,7},{15,8},{8,9},{9,10... | collective-permute-start | bytes 811016 | tf_op jit(solution)/shard_map/ppermute | solution.py:393
  106.3 9.8 %collective-permute-start.11 = (bf16[264,512]{1,0:T(8,128)(2,1)S(1)}, bf16[264,512]{1,0:T(8,128)(2,1)S(1)}, u32[]{:S(2)}, u32[]{:S(2)}) collective-permute-start(bf16[264,512]{1,0:T(8,128)(2,1)S(1)} %get-tuple-element.32), channel_id=1, source_target_pairs={{1,0},{2,1},{3,2},{4,3},{5,4},{6,5},{7,6},{0,7},{9,8},{10,9},{11,1... | collective-permute-start | bytes 811016 | tf_op jit(solution)/shard_map/ppermute | solution.py:393
  112.4 9.0 %collective-permute-start.8 = (bf16[264,512]{1,0:T(8,128)(2,1)S(1)}, bf16[264,512]{1,0:T(8,128)(2,1)S(1)}, u32[]{:S(2)}, u32[]{:S(2)}) collective-permute-start(bf16[264,512]{1,0:T(8,128)(2,1)S(1)} %add_convert_fusion.4), channel_id=1, source_target_pairs={{7,0},{0,1},{1,2},{2,3},{3,4},{4,5},{5,6},{6,7},{15,8},{8,9},{9,10... | collective-permute-start | bytes 811016 | tf_op jit(solution)/shard_map/ppermute | solution.py:393
  116.2 9.0 %collective-permute-start.12 = (bf16[264,512]{1,0:T(8,128)(2,1)S(1)}, bf16[264,512]{1,0:T(8,128)(2,1)S(1)}, u32[]{:S(2)}, u32[]{:S(2)}) collective-permute-start(bf16[264,512]{1,0:T(8,128)(2,1)S(1)} %add_convert_fusion.1), channel_id=1, source_target_pairs={{1,0},{2,1},{3,2},{4,3},{5,4},{6,5},{7,6},{0,7},{9,8},{10,9},{11,1... | collective-permute-start | bytes 811016 | tf_op jit(solution)/shard_map/ppermute | solution.py:393
  121.5 8.2 %collective-permute-start.9 = (bf16[264,512]{1,0:T(8,128)(2,1)S(1)}, bf16[264,512]{1,0:T(8,128)(2,1)S(1)}, u32[]{:S(2)}, u32[]{:S(2)}) collective-permute-start(bf16[264,512]{1,0:T(8,128)(2,1)S(1)} %add_convert_fusion.3), channel_id=1, source_target_pairs={{7,0},{0,1},{1,2},{2,3},{3,4},{4,5},{5,6},{6,7},{15,8},{8,9},{9,10... | collective-permute-start | bytes 811016 | tf_op jit(solution)/shard_map/ppermute | solution.py:393
  125.3 8.2 %collective-permute-start.13 = (bf16[264,512]{1,0:T(8,128)(2,1)S(1)}, bf16[264,512]{1,0:T(8,128)(2,1)S(1)}, u32[]{:S(2)}, u32[]{:S(2)}) collective-permute-start(bf16[264,512]{1,0:T(8,128)(2,1)S(1)} %add_convert_fusion), channel_id=1, source_target_pairs={{1,0},{2,1},{3,2},{4,3},{5,4},{6,5},{7,6},{0,7},{9,8},{10,9},{11,1... | collective-permute-start | bytes 811016 | tf_op jit(solution)/shard_map/ppermute | solution.py:393
  129.8 7.7 %collective-permute-start.10 = (bf16[264,512]{1,0:T(8,128)(2,1)S(1)}, bf16[264,512]{1,0:T(8,128)(2,1)S(1)}, u32[]{:S(2)}, u32[]{:S(2)}) collective-permute-start(bf16[264,512]{1,0:T(8,128)(2,1)S(1)} %add_convert_fusion.2), channel_id=1, source_target_pairs={{7,0},{0,1},{1,2},{2,3},{3,4},{4,5},{5,6},{6,7},{15,8},{8,9},{9,10... | collective-permute-start | bytes 811016 | tf_op jit(solution)/shard_map/ppermute | solution.py:393
  146.9 10.2 %collective-permute-start.14 = (f32[8,48]{1,0:T(8,128)S(1)}, f32[8,48]{1,0:T(8,128)S(1)}, u32[]{:S(2)}, u32[]{:S(2)}) collective-permute-start(f32[8,48]{1,0:T(8,128)S(1)} %slice.19), channel_id=1, source_target_pairs={{255,0},{0,1},{1,2},{2,3},{3,4},{4,5},{5,6},{6,7},{7,8},{8,9},{9,1... | collective-permute-start | bytes 4616 | tf_op jit(solution)/shard_map/ppermute | solution.py:393

commit v3 on v2

--- a/solution.py
+++ b/solution.py
@@ -175,30 +175,35 @@
 
 
 def expert_body(
-    got_hbm, win_ref, w_ref, out_hbm, z_hbm, err_hbm, code_ref, got_ref, out_ref, z_ref, err_ref, loads, stores, z_sems, err_sems
+    got_hbm, win_ref, w_ref, out_hbm, z_hbm, err_hbm, code_ref, got_ref, out_ref, z_ref, err_ref, loads, stores
 ):
     weights = lambda l: w_ref[l * D : (l + 1) * D, :]
     code_matrix = w_ref[LAYERS * D :, :]
     all_peers = [slice(k * EXP_PEERS, (k + 1) * EXP_PEERS) for k in range(EXP_STEPS)]
-    inputs = [pltpu.make_async_copy(got_hbm.at[p], got_ref.at[p], loads.at[k]) for k, p in enumerate(all_peers)]
-    for load in inputs:
-        load.start()
+    half_block = CHUNKS * CAP
+    parts = (slice(0, half_block), slice(2 * half_block, BLOCK), slice(half_block, 2 * half_block))
+    inputs = [
+        [
+            pltpu.make_async_copy(got_hbm.at[peers, part], got_ref.at[peers, part], loads.at[k, i])
+            for i, part in enumerate(parts)
+        ]
+        for k, peers in enumerate(all_peers)
+    ]
+    for group in inputs:
+        for load in group:
+            load.start()
     outputs = []
-    pending = {}
+
+    def save(k, i, src, dst):
+        outputs.append(pltpu.make_async_copy(src, dst, stores.at[k, i]))
+        outputs[-1].start()
+
     for k, peers in enumerate(all_peers):
         span = slice(k * EXP_ROWS, (k + 1) * EXP_ROWS)
-        buf = k % 2
-
-        def save(kind, ref, hbm, sems, l, value):
-            if (kind, buf, l) in pending:
-                pending[kind, buf, l].wait()
-            ref[buf, l] = value
-            pending[kind, buf, l] = pltpu.make_async_copy(ref.at[buf, l], hbm.at[l, span], sems.at[buf, l])
-            pending[kind, buf, l].start()
 
         def columns(half):
-            parts = [got_ref[peers, column_of(half, c), :].reshape(EXP_ROWS, LANES) for c in range(CHUNKS)]
-            return jnp.concatenate(parts, axis=1)
+            cols = [got_ref[peers, column_of(half, c), :].reshape(EXP_ROWS, LANES) for c in range(CHUNKS)]
+            return jnp.concatenate(cols, axis=1)
 
         def store_columns(half, value):
             for c in range(CHUNKS):
@@ -206,7 +211,8 @@
                     EXP_PEERS, CAP, LANES
                 )
 
-        inputs[k].wait()
+        inputs[k][0].wait()
+        inputs[k][1].wait()
         image = lax.broadcasted_iota(jnp.int32, (EXP_PEERS * WIN, EXP_ROWS), 0) + 1
         key = jnp.concatenate(
             [
@@ -223,20 +229,27 @@
         current = columns(0)
         slopes = []
         for l in range(LAYERS):
-            save("z", z_ref, z_hbm, z_sems, l, current)
-            pre = dot(current, weights(l))
+            z_ref[l, span, :] = current
             if l == 0:
-                pre = pre + dot(code_rows, code_matrix)
+                pre = dot(code_rows, code_matrix) + dot(current, weights(l))
+            else:
+                pre = dot(current, weights(l))
             s = 0.5 * jnp.tanh(0.5 * pre) + 0.5
             act = pre * s
             slopes.append(s + act * (1.0 - s))
             current = act.astype(BF16)
         store_columns(0, current)
+        inputs[k][2].wait()
+        save(k, 0, z_ref.at[:, span], z_hbm.at[:, span])
+        save(k, 1, out_ref.at[peers, parts[0]], out_hbm.at[peers, parts[0]])
         up = columns(1).astype(F32)
         for l in range(LAYERS - 1, -1, -1):
             err = (up * slopes[l]).astype(BF16)
-            save("err", err_ref, err_hbm, err_sems, l, err)
+            err_ref[l, span, :] = err
+            if l == 1:
+                save(k, 2, err_ref.at[1:, span], err_hbm.at[1:, span])
             up = dot(err, weights(l), 1, 1)
+        save(k, 3, err_ref.at[0, span], err_hbm.at[0, span])
         code_back = dot(err, code_matrix, 1, 1).astype(BF16)
         store_columns(1, up.astype(BF16))
         sums = dot(hot, code_back)
@@ -245,9 +258,9 @@
             low = sums[j * WIN : j * WIN + IMG_DEV]
             high = sums[j * WIN + IMG_DEV : (j + 1) * WIN]
             out_ref[k * EXP_PEERS + j, BLOCK - TAIL :, :] = jnp.concatenate([low, pad, high, pad], axis=1).astype(BF16)
-        outputs.append(pltpu.make_async_copy(out_ref.at[peers], out_hbm.at[peers], stores.at[k]))
-        outputs[-1].start()
-    for store in list(pending.values()) + outputs:
+        rest = slice(half_block, BLOCK)
+        save(k, 4, out_ref.at[peers, rest], out_hbm.at[peers, rest])
+    for store in outputs:
         store.wait()
 
 
@@ -259,12 +272,10 @@
         scratch_shapes=[
             pltpu.VMEM((PEERS, BLOCK, LANES), BF16),
             pltpu.VMEM((PEERS, BLOCK, LANES), BF16),
-            pltpu.VMEM((2, LAYERS, EXP_ROWS, D), BF16),
-            pltpu.VMEM((2, LAYERS, EXP_ROWS, D), BF16),
-            pltpu.SemaphoreType.DMA((EXP_STEPS,)),
-            pltpu.SemaphoreType.DMA((EXP_STEPS,)),
-            pltpu.SemaphoreType.DMA((2, LAYERS)),
-            pltpu.SemaphoreType.DMA((2, LAYERS)),
+            pltpu.VMEM((LAYERS, SLOTS, D), BF16),
+            pltpu.VMEM((LAYERS, SLOTS, D), BF16),
+            pltpu.SemaphoreType.DMA((EXP_STEPS, 3)),
+            pltpu.SemaphoreType.DMA((EXP_STEPS, 5)),
         ],
         out_shape=[
             pltpu.HBM((PEERS, BLOCK, LANES), BF16),

time: 158 us -> 157 us (level)
  no operation moved by 1% of the time
where the time goes in v3:
time: 157 us
  waiting for transfers between devices  58.7 us (37%)
  starting transfers between devices  44.8 us (29%)
  Pallas kernels  39.7 us (25%)
  local copies, waits for them, and re-layouts  10.5 us (7%)
  other arithmetic  2 us (1%)
    ppermute x15, waiting for transfers between devices, shifted(): return lax.ppermute(block, axis, route)  37.7 us
    ppermute x15, starting transfers between devices, shifted(): return lax.ppermute(block, axis, route)  32.4 us
    all_to_all x2, waiting for transfers between devices, exchange(): lax.all_to_all(values, 'expert', split_axis=0, concat_axis=0, tiled=True)  21 us
    pallas_call x1, Pallas kernels, expert(): pl.pallas_call(expert_body, in_specs=[in_hbm(), in_vmem(), in_vmem()], ou...  16.1 us
    all_to_all x2, starting transfers between devices, exchange(): lax.all_to_all(values, 'expert', split_axis=0, concat_axis=0, tiled=True)  12.4 us
    unnamed x26, local copies, waits for them, and re-layouts  9.57 us
    pallas_call x1, Pallas kernels, grads(): pl.pallas_call(grads_body, grid_spec=pltpu.PrefetchScalarGridSpec(num_sca...  8.14 us
    pallas_call x1, Pallas kernels, pack(): pl.pallas_call(pack_body, in_specs=[in_smem()] + [in_hbm()] * 4, out_spec...  6.84 us
  transfers between devices with their start and end apart: 17, of which 10 were waited for; matrix products, arithmetic and copies ran while one was open for 1% of the time, Pallas kernels for 11%

profile of v3, /device:TPU:96, one launch (start us, length us, event | category | flops | bytes accessed | tf_op | source)
XLA Modules:
  0.0 156.5 jit_solution(6543429257139961784)
XLA Ops:
  0.6 6.8 %pack.1 = (bf16[32,520,128]{2,1,0:T(8,128)(2,1)}, s32[1,1024]{1,0:T(1,128)S(1)}) custom-call(s32[1]{0:T(128)} %bitcast.first_ref, s32[1,1024]{1,0:T(1,128)} %bitcast.14, s32[1,1024]{1,0:T(1,128)} %bitcast.15, bf16[1024,512]{1,0:T(8,128)(2,1)} %feats_hbm.1, bf16[1024,512]{1,0:T(8,128)(2,1)} %cot_hbm.1), custom_call_target="tpu_custom_call" | custom-call | bytes 24000000 | tf_op jit(solution)/shard_map/pack/pallas_call | solution.py:124
  7.5 0.0 copy-start.11
  7.5 0.0 copy-start.12
  7.5 0.0 slice-start
  7.5 7.6 %all-to-all-start = ((bf16[32,520,128]{2,1,0:T(8,128)(2,1)}), bf16[32,520,128]{2,1,0:T(8,128)(2,1)}, u32[]{:S(2)}, u32[]{:S(2)}) async-start(bf16[32,520,128]{2,1,0:T(8,128)(2,1)} %get-tuple-element.23), calls=%async_computation | async-start | bytes 8519680 | tf_op jit(solution)/shard_map/all_to_all | solution.py:398
  15.1 0.0 copy-done.11
  15.1 3.2 %collective-permute-start = (bf16[264,512]{1,0:T(8,128)(2,1)S(1)}, bf16[264,512]{1,0:T(8,128)(2,1)S(1)}, u32[]{:S(2)}, u32[]{:S(2)}) collective-permute-start(bf16[264,512]{1,0:T(8,128)(2,1)S(1)} %pad.4.refs_0_), channel_id=1, source_target_pairs={{7,0},{0,1},{1,2},{2,3},{3,4},{4,5},{5,6},{6,7},{15,8},{8,9},{9,10... | collective-permute-start | bytes 811016 | tf_op jit(solution)/shard_map/ppermute | solution.py:404
  18.3 0.0 collective-permute-start.1
  18.4 6.1 %collective-permute-done.refs_1_ = bf16[264,512]{1,0:T(8,128)(2,1)S(1)} collective-permute-done((bf16[264,512]{1,0:T(8,128)(2,1)S(1)}, bf16[264,512]{1,0:T(8,128)(2,1)S(1)}, u32[]{:S(2)}, u32[]{:S(2)}) %collective-permute-start) | collective-permute-done | bytes 270368 | tf_op jit(solution)/shard_map/ppermute | solution.py:404
  24.5 3.7 %collective-permute-start.2 = (bf16[264,512]{1,0:T(8,128)(2,1)S(1)}, bf16[264,512]{1,0:T(8,128)(2,1)S(1)}, u32[]{:S(2)}, u32[]{:S(2)}) collective-permute-start(bf16[264,512]{1,0:T(8,128)(2,1)S(1)} %collective-permute-done.refs_1_), channel_id=1, source_target_pairs={{7,0},{0,1},{1,2},{2,3},{3,4},{4,5},{5,6},{6,7},{15,8},{8,9},{9,10... | collective-permute-start | bytes 811016 | tf_op jit(solution)/shard_map/ppermute | solution.py:404
  28.2 0.0 collective-permute-done.1.refs_2_
  28.2 0.0 collective-permute-start.3
  28.2 5.4 %collective-permute-done.2.refs_3_ = bf16[264,512]{1,0:T(8,128)(2,1)S(1)} collective-permute-done((bf16[264,512]{1,0:T(8,128)(2,1)S(1)}, bf16[264,512]{1,0:T(8,128)(2,1)S(1)}, u32[]{:S(2)}, u32[]{:S(2)}) %collective-permute-start.2) | collective-permute-done | bytes 270368 | tf_op jit(solution)/shard_map/ppermute | solution.py:404
  33.6 3.7 %collective-permute-start.4 = (bf16[264,512]{1,0:T(8,128)(2,1)S(1)}, bf16[264,512]{1,0:T(8,128)(2,1)S(1)}, u32[]{:S(2)}, u32[]{:S(2)}) collective-permute-start(bf16[264,512]{1,0:T(8,128)(2,1)S(1)} %collective-permute-done.2.refs_3_), channel_id=1, source_target_pairs={{7,0},{0,1},{1,2},{2,3},{3,4},{4,5},{5,6},{6,7},{15,8},{8,9},{9,10... | collective-permute-start | bytes 811016 | tf_op jit(solution)/shard_map/ppermute | solution.py:404
  37.3 0.0 collective-permute-done.3.refs_4_
  37.3 0.0 collective-permute-start.5
  37.3 4.6 %collective-permute-done.4.refs_5_ = bf16[264,512]{1,0:T(8,128)(2,1)S(1)} collective-permute-done((bf16[264,512]{1,0:T(8,128)(2,1)S(1)}, bf16[264,512]{1,0:T(8,128)(2,1)S(1)}, u32[]{:S(2)}, u32[]{:S(2)}) %collective-permute-start.4) | collective-permute-done | bytes 270368 | tf_op jit(solution)/shard_map/ppermute | solution.py:404
  41.8 3.7 %collective-permute-start.6 = (bf16[264,512]{1,0:T(8,128)(2,1)S(1)}, bf16[264,512]{1,0:T(8,128)(2,1)S(1)}, u32[]{:S(2)}, u32[]{:S(2)}) collective-permute-start(bf16[264,512]{1,0:T(8,128)(2,1)S(1)} %collective-permute-done.4.refs_5_), channel_id=1, source_target_pairs={{7,0},{0,1},{1,2},{2,3},{3,4},{4,5},{5,6},{6,7},{15,8},{8,9},{9,10... | collective-permute-start | bytes 811016 | tf_op jit(solution)/shard_map/ppermute | solution.py:404
  45.5 0.2 fusion
  45.7 0.4 reshape.30
  46.1 0.5 copy.10
  46.6 0.0 collective-permute-done.5.refs_6_
  46.6 0.7 copy-done.7
  47.3 2.2 %collective-permute-done.6.refs_7_ = bf16[264,512]{1,0:T(8,128)(2,1)S(1)} collective-permute-done((bf16[264,512]{1,0:T(8,128)(2,1)S(1)}, bf16[264,512]{1,0:T(8,128)(2,1)S(1)}, u32[]{:S(2)}, u32[]{:S(2)}) %collective-permute-start.6) | collective-permute-done | bytes 270368 | tf_op jit(solution)/shard_map/ppermute | solution.py:404
  49.5 0.7 copy-done.9
  50.2 1.0 copy-done.2
  51.2 1.0 copy-done.4
  52.1 1.0 copy-done.6
  53.1 1.0 copy-done.8
  54.0 1.0 copy-done.10
  55.0 0.8 join.1.w_ref
  55.8 13.7 %all-to-all-done.got_hbm = bf16[32,520,128]{2,1,0:T(8,128)(2,1)} async-done(((bf16[32,520,128]{2,1,0:T(8,128)(2,1)}), bf16[32,520,128]{2,1,0:T(8,128)(2,1)}, u32[]{:S(2)}, u32[]{:S(2)}) %all-to-all-start) | async-done | bytes 4259872 | tf_op jit(solution)/shard_map/all_to_all | solution.py:398
  69.4 16.1 %expert.1 = (bf16[32,520,128]{2,1,0:T(8,128)(2,1)}, bf16[4,2048,512]{2,1,0:T(8,128)(2,1)}, bf16[4,2048,512]{2,1,0:T(8,128)(2,1)}, bf16[2048,48]{1,0:T(8,128)(2,1)S(1)}) custom-call(bf16[32,520,128]{2,1,0:T(8,128)(2,1)} %all-to-all-done.got_hbm, bf16[512,48]{1,0:T(8,128)(2,1)S(1)} %bitcast.10, bf16[2096,512]{1,0:T(8,128)(2,1)S(1)} %join.1.w_ref), custom_call_target="tpu_custom_call" | custom-call | bytes 51000000 | tf_op jit(solution)/shard_map/expert/pallas_call | solution.py:268
  85.6 4.9 %all-to-all-start.1 = ((bf16[32,520,128]{2,1,0:T(8,128)(2,1)}), bf16[32,520,128]{2,1,0:T(8,128)(2,1)}, u32[]{:S(2)}, u32[]{:S(2)}) async-start(bf16[32,520,128]{2,1,0:T(8,128)(2,1)} %get-tuple-element.24), calls=%async_computation.1 | async-start | bytes 8519680 | tf_op jit(solution)/shard_map/all_to_all | solution.py:398
  90.4 0.0 copy-start
  90.4 3.4 %copy-done = bf16[4,2048,512]{2,1,0:T(8,128)(2,1)S(1)} copy-done((bf16[4,2048,512]{2,1,0:T(8,128)(2,1)S(1)}, bf16[4,2048,512]{2,1,0:T(8,128)(2,1)}, u32[]{:S(2)}) %copy-start) | copy-done | bytes 8388632
  93.8 8.1 %grads.1 = (bf16[264,512]{1,0:T(8,128)(2,1)S(1)}, bf16[264,512]{1,0:T(8,128)(2,1)S(1)}, bf16[264,512]{1,0:T(8,128)(2,1)S(1)}, bf16[264,512]{1,0:T(8,128)(2,1)S(1...) custom-call(s32[1]{0:T(128)} %bitcast.4.narrow_ref, ...), custom_call_target="tpu_custom_call" | custom-call | bytes 30000000 | tf_op jit(solution)/shard_map/grads/pallas_call | solution.py:312
  101.9 3.2 %collective-permute-start.7 = (bf16[264,512]{1,0:T(8,128)(2,1)S(1)}, bf16[264,512]{1,0:T(8,128)(2,1)S(1)}, u32[]{:S(2)}, u32[]{:S(2)}) collective-permute-start(bf16[264,512]{1,0:T(8,128)(2,1)S(1)} %get-tuple-element.28), channel_id=1, source_target_pairs={{7,0},{0,1},{1,2},{2,3},{3,4},{4,5},{5,6},{6,7},{15,8},{8,9},{9,10... | collective-permute-start | bytes 811016 | tf_op jit(solution)/shard_map/ppermute | solution.py:404
  105.1 0.0 collective-permute-start.11
  105.1 6.0 %collective-permute-done.7 = bf16[264,512]{1,0:T(8,128)(2,1)S(1)} collective-permute-done((bf16[264,512]{1,0:T(8,128)(2,1)S(1)}, bf16[264,512]{1,0:T(8,128)(2,1)S(1)}, u32[]{:S(2)}, u32[]{:S(2)}) %collective-permute-start.7) | collective-permute-done | bytes 270368 | tf_op jit(solution)/shard_map/ppermute | solution.py:404
  111.1 0.1 add_convert_fusion.4
  111.2 3.8 %collective-permute-start.8 = (bf16[264,512]{1,0:T(8,128)(2,1)S(1)}, bf16[264,512]{1,0:T(8,128)(2,1)S(1)}, u32[]{:S(2)}, u32[]{:S(2)}) collective-permute-start(bf16[264,512]{1,0:T(8,128)(2,1)S(1)} %add_convert_fusion.4), channel_id=1, source_target_pairs={{7,0},{0,1},{1,2},{2,3},{3,4},{4,5},{5,6},{6,7},{15,8},{8,9},{9,10... | collective-permute-start | bytes 811016 | tf_op jit(solution)/shard_map/ppermute | solution.py:404
  115.0 0.0 collective-permute-done.11
  115.0 0.1 add_convert_fusion.1
  115.1 0.1 collective-permute-start.12
  115.2 5.1 %collective-permute-done.8 = bf16[264,512]{1,0:T(8,128)(2,1)S(1)} collective-permute-done((bf16[264,512]{1,0:T(8,128)(2,1)S(1)}, bf16[264,512]{1,0:T(8,128)(2,1)S(1)}, u32[]{:S(2)}, u32[]{:S(2)}) %collective-permute-start.8) | collective-permute-done | bytes 270368 | tf_op jit(solution)/shard_map/ppermute | solution.py:404
  120.3 0.1 add_convert_fusion.3
  120.3 3.8 %collective-permute-start.9 = (bf16[264,512]{1,0:T(8,128)(2,1)S(1)}, bf16[264,512]{1,0:T(8,128)(2,1)S(1)}, u32[]{:S(2)}, u32[]{:S(2)}) collective-permute-start(bf16[264,512]{1,0:T(8,128)(2,1)S(1)} %add_convert_fusion.3), channel_id=1, source_target_pairs={{7,0},{0,1},{1,2},{2,3},{3,4},{4,5},{5,6},{6,7},{15,8},{8,9},{9,10... | collective-permute-start | bytes 811016 | tf_op jit(solution)/shard_map/ppermute | solution.py:404
  124.1 0.0 collective-permute-done.12
  124.1 0.1 add_convert_fusion
  124.2 0.1 collective-permute-start.13
  124.3 4.3 %collective-permute-done.9 = bf16[264,512]{1,0:T(8,128)(2,1)S(1)} collective-permute-done((bf16[264,512]{1,0:T(8,128)(2,1)S(1)}, bf16[264,512]{1,0:T(8,128)(2,1)S(1)}, u32[]{:S(2)}, u32[]{:S(2)}) %collective-permute-start.9) | collective-permute-done | bytes 270368 | tf_op jit(solution)/shard_map/ppermute | solution.py:404
  128.6 0.1 add_convert_fusion.2
  128.6 3.8 %collective-permute-start.10 = (bf16[264,512]{1,0:T(8,128)(2,1)S(1)}, bf16[264,512]{1,0:T(8,128)(2,1)S(1)}, u32[]{:S(2)}, u32[]{:S(2)}) collective-permute-start(bf16[264,512]{1,0:T(8,128)(2,1)S(1)} %add_convert_fusion.2), channel_id=1, source_target_pairs={{7,0},{0,1},{1,2},{2,3},{3,4},{4,5},{5,6},{6,7},{15,8},{8,9},{9,10... | collective-permute-start | bytes 811016 | tf_op jit(solution)/shard_map/ppermute | solution.py:404
  132.4 0.0 collective-permute-done.13.b_ref
  132.4 4.0 %collective-permute-done.10.a_ref = bf16[264,512]{1,0:T(8,128)(2,1)S(1)} collective-permute-done((bf16[264,512]{1,0:T(8,128)(2,1)S(1)}, bf16[264,512]{1,0:T(8,128)(2,1)S(1)}, u32[]{:S(2)}, u32[]{:S(2)}) %collective-permute-start.10) | collective-permute-done | bytes 270368 | tf_op jit(solution)/shard_map/ppermute | solution.py:404
  136.4 1.0 finish.1
  137.3 7.4 %all-to-all-done.1.back_hbm = bf16[32,520,128]{2,1,0:T(8,128)(2,1)} async-done(((bf16[32,520,128]{2,1,0:T(8,128)(2,1)}), bf16[32,520,128]{2,1,0:T(8,128)(2,1)}, u32[]{:S(2)}, u32[]{:S(2)}) %all-to-all-start.1) | async-done | bytes 4259872 | tf_op jit(solution)/shard_map/all_to_all | solution.py:398
  144.7 0.9 convert_reduce_fusion
  145.6 0.1 slice.19
  145.7 3.4 %collective-permute-start.14 = (f32[8,48]{1,0:T(8,128)S(1)}, f32[8,48]{1,0:T(8,128)S(1)}, u32[]{:S(2)}, u32[]{:S(2)}) collective-permute-start(f32[8,48]{1,0:T(8,128)S(1)} %slice.19), channel_id=1, source_target_pairs={{255,0},{0,1},{1,2},{2,3},{3,4},{4,5},{5,6},{6,7},{7,8},{8,9},{9,1... | collective-permute-start | bytes 4616 | tf_op jit(solution)/shard_map/ppermute | solution.py:404
  149.1 6.8 %unpack.1 = (bf16[1024,512]{1,0:T(8,128)(2,1)}, bf16[1024,512]{1,0:T(8,128)(2,1)}) custom-call(s32[1,1024]{1,0:T(1,128)S(1)} %get-tuple-element.22.pos_ref, bf16[32,520,128]{2,1,0:T(8,128)(2,1)} %all-to-all-done.1.back_hbm), custom_call_target="tpu_custom_call" | custom-call | bytes 21000000 | tf_op jit(solution)/shard_map/unpack/pallas_call | solution.py:377
  155.9 0.0 collective-permute-done.14
  155.9 0.6 slice_add_fusion
  (16 shorter events, 0.0 us)
Async XLA Ops:
  7.5 7.6 %copy-start.11 = (bf16[1,262,512]{2,1,0:T(8,128)(2,1)S(1)}, bf16[1,262,512]{2,1,0:T(8,128)(2,1)}, u32[]{:S(2)}) copy-start(bf16[1,262,512]{2,1,0:T(8,128)(2,1)} %param.11) | copy-start | bytes 804868
  7.5 38.0 %copy-start.12 = (bf16[2048,48]{0,1:T(8,128)(2,1)S(1)}, bf16[2048,48]{0,1:T(8,128)(2,1)}, u32[]{:S(2)}) copy-start(bf16[2048,48]{0,1:T(8,128)(2,1)} %param.10) | copy-start | bytes 589828
  7.5 38.0 %slice-start = ((bf16[2048,48]{0,1:T(8,128)(2,1)}), bf16[64,48]{0,1:T(8,128)(2,1)S(1)}, s32[]{:S(2)}) async-start(bf16[2048,48]{0,1:T(8,128)(2,1)} %param.10), calls=%async_computation.2 | async-start | bytes 24576 | tf_op jit(solution)/shard_map/slice | solution.py:461
  7.5 61.9 %all-to-all-start = ((bf16[32,520,128]{2,1,0:T(8,128)(2,1)}), bf16[32,520,128]{2,1,0:T(8,128)(2,1)}, u32[]{:S(2)}, u32[]{:S(2)}) async-start(bf16[32,520,128]{2,1,0:T(8,128)(2,1)} %get-tuple-element.23), calls=%async_computation | async-start | bytes 8519680 | tf_op jit(solution)/shard_map/all_to_all | solution.py:398
  15.1 9.3 %collective-permute-start = (bf16[264,512]{1,0:T(8,128)(2,1)S(1)}, bf16[264,512]{1,0:T(8,128)(2,1)S(1)}, u32[]{:S(2)}, u32[]{:S(2)}) collective-permute-start(bf16[264,512]{1,0:T(8,128)(2,1)S(1)} %pad.4.refs_0_), channel_id=1, source_target_pairs={{7,0},{0,1},{1,2},{2,3},{3,4},{4,5},{5,6},{6,7},{15,8},{8,9},{9,10... | collective-permute-start | bytes 811016 | tf_op jit(solution)/shard_map/ppermute | solution.py:404
  18.3 9.8 %collective-permute-start.1 = (bf16[264,512]{1,0:T(8,128)(2,1)S(1)}, bf16[264,512]{1,0:T(8,128)(2,1)S(1)}, u32[]{:S(2)}, u32[]{:S(2)}) collective-permute-start(bf16[264,512]{1,0:T(8,128)(2,1)S(1)} %pad.4.refs_0_), channel_id=1, source_target_pairs={{1,0},{2,1},{3,2},{4,3},{5,4},{6,5},{7,6},{0,7},{9,8},{10,9},{11,1... | collective-permute-start | bytes 811016 | tf_op jit(solution)/shard_map/ppermute | solution.py:404
  24.5 9.1 %collective-permute-start.2 = (bf16[264,512]{1,0:T(8,128)(2,1)S(1)}, bf16[264,512]{1,0:T(8,128)(2,1)S(1)}, u32[]{:S(2)}, u32[]{:S(2)}) collective-permute-start(bf16[264,512]{1,0:T(8,128)(2,1)S(1)} %collective-permute-done.refs_1_), channel_id=1, source_target_pairs={{7,0},{0,1},{1,2},{2,3},{3,4},{4,5},{5,6},{6,7},{15,8},{8,9},{9,10... | collective-permute-start | bytes 811016 | tf_op jit(solution)/shard_map/ppermute | solution.py:404
  28.2 9.1 %collective-permute-start.3 = (bf16[264,512]{1,0:T(8,128)(2,1)S(1)}, bf16[264,512]{1,0:T(8,128)(2,1)S(1)}, u32[]{:S(2)}, u32[]{:S(2)}) collective-permute-start(bf16[264,512]{1,0:T(8,128)(2,1)S(1)} %collective-permute-done.1.refs_2_), channel_id=1, source_target_pairs={{1,0},{2,1},{3,2},{4,3},{5,4},{6,5},{7,6},{0,7},{9,8},{10,9},{11,1... | collective-permute-start | bytes 811016 | tf_op jit(solution)/shard_map/ppermute | solution.py:404
  33.6 12.5 %copy-start.1 = (bf16[264,512]{1,0:T(8,128)(2,1)}, bf16[264,512]{1,0:T(8,128)(2,1)S(1)}, u32[]{:S(2)}) copy-start(bf16[264,512]{1,0:T(8,128)(2,1)S(1)} %collective-permute-done.2.refs_3_) | copy-start | bytes 811012
  33.6 8.3 %collective-permute-start.4 = (bf16[264,512]{1,0:T(8,128)(2,1)S(1)}, bf16[264,512]{1,0:T(8,128)(2,1)S(1)}, u32[]{:S(2)}, u32[]{:S(2)}) collective-permute-start(bf16[264,512]{1,0:T(8,128)(2,1)S(1)} %collective-permute-done.2.refs_3_), channel_id=1, source_target_pairs={{7,0},{0,1},{1,2},{2,3},{3,4},{4,5},{5,6},{6,7},{15,8},{8,9},{9,10... | collective-permute-start | bytes 811016 | tf_op jit(solution)/shard_map/ppermute | solution.py:404
  37.3 12.3 %copy-start.3 = (bf16[264,512]{1,0:T(8,128)(2,1)}, bf16[264,512]{1,0:T(8,128)(2,1)S(1)}, u32[]{:S(2)}) copy-start(bf16[264,512]{1,0:T(8,128)(2,1)S(1)} %collective-permute-done.3.refs_4_) | copy-start | bytes 811012
  37.3 9.3 %collective-permute-start.5 = (bf16[264,512]{1,0:T(8,128)(2,1)S(1)}, bf16[264,512]{1,0:T(8,128)(2,1)S(1)}, u32[]{:S(2)}, u32[]{:S(2)}) collective-permute-start(bf16[264,512]{1,0:T(8,128)(2,1)S(1)} %collective-permute-done.3.refs_4_), channel_id=1, source_target_pairs={{1,0},{2,1},{3,2},{4,3},{5,4},{6,5},{7,6},{0,7},{9,8},{10,9},{11,1... | collective-permute-start | bytes 811016 | tf_op jit(solution)/shard_map/ppermute | solution.py:404
  41.8 7.7 %copy-start.5 = (bf16[264,512]{1,0:T(8,128)(2,1)}, bf16[264,512]{1,0:T(8,128)(2,1)S(1)}, u32[]{:S(2)}) copy-start(bf16[264,512]{1,0:T(8,128)(2,1)S(1)} %collective-permute-done.4.refs_5_) | copy-start | bytes 811012
  41.8 7.7 %collective-permute-start.6 = (bf16[264,512]{1,0:T(8,128)(2,1)S(1)}, bf16[264,512]{1,0:T(8,128)(2,1)S(1)}, u32[]{:S(2)}, u32[]{:S(2)}) collective-permute-start(bf16[264,512]{1,0:T(8,128)(2,1)S(1)} %collective-permute-done.4.refs_5_), channel_id=1, source_target_pairs={{7,0},{0,1},{1,2},{2,3},{3,4},{4,5},{5,6},{6,7},{15,8},{8,9},{9,10... | collective-permute-start | bytes 811016 | tf_op jit(solution)/shard_map/ppermute | solution.py:404
  46.6 0.7 copy-start.7
  49.5 0.7 copy-start.9
  50.2 1.0 copy-start.2
  51.2 1.0 copy-start.4
  52.1 1.0 copy-start.6
  53.1 1.0 copy-start.8
  54.0 1.0 copy-start.10
  85.6 59.2 %all-to-all-start.1 = ((bf16[32,520,128]{2,1,0:T(8,128)(2,1)}), bf16[32,520,128]{2,1,0:T(8,128)(2,1)}, u32[]{:S(2)}, u32[]{:S(2)}) async-start(bf16[32,520,128]{2,1,0:T(8,128)(2,1)} %get-tuple-element.24), calls=%async_computation.1 | async-start | bytes 8519680 | tf_op jit(solution)/shard_map/all_to_all | solution.py:398
  90.4 3.4 %copy-start = (bf16[4,2048,512]{2,1,0:T(8,128)(2,1)S(1)}, bf16[4,2048,512]{2,1,0:T(8,128)(2,1)}, u32[]{:S(2)}) copy-start(bf16[4,2048,512]{2,1,0:T(8,128)(2,1)} %get-tuple-element.25.z_ref) | copy-start | bytes 25165828
  101.9 9.2 %collective-permute-start.7 = (bf16[264,512]{1,0:T(8,128)(2,1)S(1)}, bf16[264,512]{1,0:T(8,128)(2,1)S(1)}, u32[]{:S(2)}, u32[]{:S(2)}) collective-permute-start(bf16[264,512]{1,0:T(8,128)(2,1)S(1)} %get-tuple-element.28), channel_id=1, source_target_pairs={{7,0},{0,1},{1,2},{2,3},{3,4},{4,5},{5,6},{6,7},{15,8},{8,9},{9,10... | collective-permute-start | bytes 811016 | tf_op jit(solution)/shard_map/ppermute | solution.py:404
  105.1 9.8 %collective-permute-start.11 = (bf16[264,512]{1,0:T(8,128)(2,1)S(1)}, bf16[264,512]{1,0:T(8,128)(2,1)S(1)}, u32[]{:S(2)}, u32[]{:S(2)}) collective-permute-start(bf16[264,512]{1,0:T(8,128)(2,1)S(1)} %get-tuple-element.32), channel_id=1, source_target_pairs={{1,0},{2,1},{3,2},{4,3},{5,4},{6,5},{7,6},{0,7},{9,8},{10,9},{11,1... | collective-permute-start | bytes 811016 | tf_op jit(solution)/shard_map/ppermute | solution.py:404
  111.2 9.0 %collective-permute-start.8 = (bf16[264,512]{1,0:T(8,128)(2,1)S(1)}, bf16[264,512]{1,0:T(8,128)(2,1)S(1)}, u32[]{:S(2)}, u32[]{:S(2)}) collective-permute-start(bf16[264,512]{1,0:T(8,128)(2,1)S(1)} %add_convert_fusion.4), channel_id=1, source_target_pairs={{7,0},{0,1},{1,2},{2,3},{3,4},{4,5},{5,6},{6,7},{15,8},{8,9},{9,10... | collective-permute-start | bytes 811016 | tf_op jit(solution)/shard_map/ppermute | solution.py:404
  115.1 9.0 %collective-permute-start.12 = (bf16[264,512]{1,0:T(8,128)(2,1)S(1)}, bf16[264,512]{1,0:T(8,128)(2,1)S(1)}, u32[]{:S(2)}, u32[]{:S(2)}) collective-permute-start(bf16[264,512]{1,0:T(8,128)(2,1)S(1)} %add_convert_fusion.1), channel_id=1, source_target_pairs={{1,0},{2,1},{3,2},{4,3},{5,4},{6,5},{7,6},{0,7},{9,8},{10,9},{11,1... | collective-permute-start | bytes 811016 | tf_op jit(solution)/shard_map/ppermute | solution.py:404
  120.3 8.2 %collective-permute-start.9 = (bf16[264,512]{1,0:T(8,128)(2,1)S(1)}, bf16[264,512]{1,0:T(8,128)(2,1)S(1)}, u32[]{:S(2)}, u32[]{:S(2)}) collective-permute-start(bf16[264,512]{1,0:T(8,128)(2,1)S(1)} %add_convert_fusion.3), channel_id=1, source_target_pairs={{7,0},{0,1},{1,2},{2,3},{3,4},{4,5},{5,6},{6,7},{15,8},{8,9},{9,10... | collective-permute-start | bytes 811016 | tf_op jit(solution)/shard_map/ppermute | solution.py:404
  124.2 8.2 %collective-permute-start.13 = (bf16[264,512]{1,0:T(8,128)(2,1)S(1)}, bf16[264,512]{1,0:T(8,128)(2,1)S(1)}, u32[]{:S(2)}, u32[]{:S(2)}) collective-permute-start(bf16[264,512]{1,0:T(8,128)(2,1)S(1)} %add_convert_fusion), channel_id=1, source_target_pairs={{1,0},{2,1},{3,2},{4,3},{5,4},{6,5},{7,6},{0,7},{9,8},{10,9},{11,1... | collective-permute-start | bytes 811016 | tf_op jit(solution)/shard_map/ppermute | solution.py:404
  128.6 7.7 %collective-permute-start.10 = (bf16[264,512]{1,0:T(8,128)(2,1)S(1)}, bf16[264,512]{1,0:T(8,128)(2,1)S(1)}, u32[]{:S(2)}, u32[]{:S(2)}) collective-permute-start(bf16[264,512]{1,0:T(8,128)(2,1)S(1)} %add_convert_fusion.2), channel_id=1, source_target_pairs={{7,0},{0,1},{1,2},{2,3},{3,4},{4,5},{5,6},{6,7},{15,8},{8,9},{9,10... | collective-permute-start | bytes 811016 | tf_op jit(solution)/shard_map/ppermute | solution.py:404
  145.7 10.2 %collective-permute-start.14 = (f32[8,48]{1,0:T(8,128)S(1)}, f32[8,48]{1,0:T(8,128)S(1)}, u32[]{:S(2)}, u32[]{:S(2)}) collective-permute-start(f32[8,48]{1,0:T(8,128)S(1)} %slice.19), channel_id=1, source_target_pairs={{255,0},{0,1},{1,2},{2,3},{3,4},{4,5},{5,6},{6,7},{7,8},{8,9},{9,1... | collective-permute-start | bytes 4616 | tf_op jit(solution)/shard_map/ppermute | solution.py:404

commit v4 on v3

--- a/solution.py
+++ b/solution.py
@@ -467,8 +467,9 @@
     back, mine = lax.optimization_barrier((back, mine))
     param_grad = mine.transpose(1, 0, 2)
     sums = jnp.sum(back[:, BLOCK - TAIL :, :].astype(F32), axis=0)
+    out_rows, feat_grad = unpack(pos, back)
+    out_rows, feat_grad, sums = lax.optimization_barrier((out_rows, feat_grad, sums))
     high = shifted(sums[:, LANES // 2 : LANES // 2 + CODE], ("expert", "narrow"), 1)
-    out_rows, feat_grad = unpack(pos, back)
     return (out_rows, feat_grad, param_grad, sums[:, :CODE] + high)
 
 

time: 157 us -> 162 us (1.032)
  the two profiles are of different devices: /device:TPU:96 before, /device:TPU:1 now
where the time goes in v4:
time: 162 us
  waiting for transfers between devices  67.3 us (42%)
  starting transfers between devices  41.4 us (26%)
  Pallas kernels  39.7 us (25%)
  local copies, waits for them, and re-layouts  10.5 us (6%)
  other arithmetic  2.01 us (1%)
    ppermute x15, waiting for transfers between devices, shifted(): return lax.ppermute(block, axis, route)  55.7 us
    ppermute x15, starting transfers between devices, shifted(): return lax.ppermute(block, axis, route)  24.5 us
    all_to_all x2, starting transfers between devices, exchange(): lax.all_to_all(values, 'expert', split_axis=0, concat_axis=0, tiled=True)  16.9 us
    pallas_call x1, Pallas kernels, expert(): pl.pallas_call(expert_body, in_specs=[in_hbm(), in_vmem(), in_vmem()], ou...  16.1 us
    all_to_all x2, waiting for transfers between devices, exchange(): lax.all_to_all(values, 'expert', split_axis=0, concat_axis=0, tiled=True)  11.6 us
    unnamed x26, local copies, waits for them, and re-layouts  9.58 us
    pallas_call x1, Pallas kernels, grads(): pl.pallas_call(grads_body, grid_spec=pltpu.PrefetchScalarGridSpec(num_sca...  8.13 us
    pallas_call x1, Pallas kernels, pack(): pl.pallas_call(pack_body, in_specs=[in_smem()] + [in_hbm()] * 4, out_spec...  6.84 us
  transfers between devices with their start and end apart: 17, of which 11 were waited for; matrix products, arithmetic and copies ran while one was open for 1% of the time, Pallas kernels for 6%

profile of v4, /device:TPU:1, one launch (start us, length us, event | category | flops | bytes accessed | tf_op | source)
XLA Modules:
  0.0 161.7 jit_solution(18272370011628618099)
XLA Ops:
  0.6 6.8 %pack.1 = (bf16[32,520,128]{2,1,0:T(8,128)(2,1)}, s32[1,1024]{1,0:T(1,128)S(1)}) custom-call(s32[1]{0:T(128)} %bitcast.first_ref, s32[1,1024]{1,0:T(1,128)} %bitcast.14, s32[1,1024]{1,0:T(1,128)} %bitcast.15, bf16[1024,512]{1,0:T(8,128)(2,1)} %feats_hbm.1, bf16[1024,512]{1,0:T(8,128)(2,1)} %cot_hbm.1), custom_call_target="tpu_custom_call" | custom-call | bytes 24000000 | tf_op jit(solution)/shard_map/pack/pallas_call | solution.py:124
  7.5 0.0 copy-start.11
  7.5 0.0 copy-start.12
  7.5 0.0 slice-start
  7.5 8.8 %all-to-all-start = ((bf16[32,520,128]{2,1,0:T(8,128)(2,1)}), bf16[32,520,128]{2,1,0:T(8,128)(2,1)}, u32[]{:S(2)}, u32[]{:S(2)}) async-start(bf16[32,520,128]{2,1,0:T(8,128)(2,1)} %get-tuple-element.26), calls=%async_computation | async-start | bytes 8519680 | tf_op jit(solution)/shard_map/all_to_all | solution.py:398
  16.3 1.7 %collective-permute-start = (bf16[264,512]{1,0:T(8,128)(2,1)S(1)}, bf16[264,512]{1,0:T(8,128)(2,1)S(1)}, u32[]{:S(2)}, u32[]{:S(2)}) collective-permute-start(bf16[264,512]{1,0:T(8,128)(2,1)S(1)} %pad.4.refs_0_), channel_id=1, source_target_pairs={{7,0},{0,1},{1,2},{2,3},{3,4},{4,5},{5,6},{6,7},{15,8},{8,9},{9,10... | collective-permute-start | bytes 811016 | tf_op jit(solution)/shard_map/ppermute | solution.py:404
  18.1 4.0 %collective-permute-start.1 = (bf16[264,512]{1,0:T(8,128)(2,1)S(1)}, bf16[264,512]{1,0:T(8,128)(2,1)S(1)}, u32[]{:S(2)}, u32[]{:S(2)}) collective-permute-start(bf16[264,512]{1,0:T(8,128)(2,1)S(1)} %pad.4.refs_0_), channel_id=1, source_target_pairs={{1,0},{2,1},{3,2},{4,3},{5,4},{6,5},{7,6},{0,7},{9,8},{10,9},{11,1... | collective-permute-start | bytes 811016 | tf_op jit(solution)/shard_map/ppermute | solution.py:404
  22.1 6.7 %collective-permute-done.refs_1_ = bf16[264,512]{1,0:T(8,128)(2,1)S(1)} collective-permute-done((bf16[264,512]{1,0:T(8,128)(2,1)S(1)}, bf16[264,512]{1,0:T(8,128)(2,1)S(1)}, u32[]{:S(2)}, u32[]{:S(2)}) %collective-permute-start) | collective-permute-done | bytes 270368 | tf_op jit(solution)/shard_map/ppermute | solution.py:404
  28.7 0.0 collective-permute-start.2
  28.7 0.0 collective-permute-done.1.refs_2_
  28.7 2.7 %collective-permute-start.3 = (bf16[264,512]{1,0:T(8,128)(2,1)S(1)}, bf16[264,512]{1,0:T(8,128)(2,1)S(1)}, u32[]{:S(2)}, u32[]{:S(2)}) collective-permute-start(bf16[264,512]{1,0:T(8,128)(2,1)S(1)} %collective-permute-done.1.refs_2_), channel_id=1, source_target_pairs={{1,0},{2,1},{3,2},{4,3},{5,4},{6,5},{7,6},{0,7},{9,8},{10,9},{11,1... | collective-permute-start | bytes 811016 | tf_op jit(solution)/shard_map/ppermute | solution.py:404
  31.4 6.0 %collective-permute-done.2.refs_3_ = bf16[264,512]{1,0:T(8,128)(2,1)S(1)} collective-permute-done((bf16[264,512]{1,0:T(8,128)(2,1)S(1)}, bf16[264,512]{1,0:T(8,128)(2,1)S(1)}, u32[]{:S(2)}, u32[]{:S(2)}) %collective-permute-start.2) | collective-permute-done | bytes 270368 | tf_op jit(solution)/shard_map/ppermute | solution.py:404
  37.4 0.0 collective-permute-start.4
  37.4 0.0 collective-permute-done.3.refs_4_
  37.4 0.0 copy-start.3
  37.4 2.7 %collective-permute-start.5 = (bf16[264,512]{1,0:T(8,128)(2,1)S(1)}, bf16[264,512]{1,0:T(8,128)(2,1)S(1)}, u32[]{:S(2)}, u32[]{:S(2)}) collective-permute-start(bf16[264,512]{1,0:T(8,128)(2,1)S(1)} %collective-permute-done.3.refs_4_), channel_id=1, source_target_pairs={{1,0},{2,1},{3,2},{4,3},{5,4},{6,5},{7,6},{0,7},{9,8},{10,9},{11,1... | collective-permute-start | bytes 811016 | tf_op jit(solution)/shard_map/ppermute | solution.py:404
  40.1 5.1 %collective-permute-done.4.refs_5_ = bf16[264,512]{1,0:T(8,128)(2,1)S(1)} collective-permute-done((bf16[264,512]{1,0:T(8,128)(2,1)S(1)}, bf16[264,512]{1,0:T(8,128)(2,1)S(1)}, u32[]{:S(2)}, u32[]{:S(2)}) %collective-permute-start.4) | collective-permute-done | bytes 270368 | tf_op jit(solution)/shard_map/ppermute | solution.py:404
  45.2 0.0 collective-permute-start.6
  45.2 0.0 slice-done
  45.2 0.2 fusion
  45.4 0.4 reshape.30
  45.8 0.5 copy.10
  46.3 0.0 collective-permute-done.5.refs_6_
  46.3 0.7 copy-done.7
  47.0 5.2 %collective-permute-done.6.refs_7_ = bf16[264,512]{1,0:T(8,128)(2,1)S(1)} collective-permute-done((bf16[264,512]{1,0:T(8,128)(2,1)S(1)}, bf16[264,512]{1,0:T(8,128)(2,1)S(1)}, u32[]{:S(2)}, u32[]{:S(2)}) %collective-permute-start.6) | collective-permute-done | bytes 270368 | tf_op jit(solution)/shard_map/ppermute | solution.py:404
  52.2 0.7 copy-done.9
  52.9 1.0 copy-done.2
  53.9 1.0 copy-done.4
  54.8 1.0 copy-done.6
  55.8 1.0 copy-done.8
  56.7 1.0 copy-done.10
  57.7 0.8 join.1.w_ref
  58.5 8.8 %all-to-all-done.got_hbm = bf16[32,520,128]{2,1,0:T(8,128)(2,1)} async-done(((bf16[32,520,128]{2,1,0:T(8,128)(2,1)}), bf16[32,520,128]{2,1,0:T(8,128)(2,1)}, u32[]{:S(2)}, u32[]{:S(2)}) %all-to-all-start) | async-done | bytes 4259872 | tf_op jit(solution)/shard_map/all_to_all | solution.py:398
  67.2 16.1 %expert.1 = (bf16[32,520,128]{2,1,0:T(8,128)(2,1)}, bf16[4,2048,512]{2,1,0:T(8,128)(2,1)}, bf16[4,2048,512]{2,1,0:T(8,128)(2,1)}, bf16[2048,48]{1,0:T(8,128)(2,1)S(1)}) custom-call(bf16[32,520,128]{2,1,0:T(8,128)(2,1)} %all-to-all-done.got_hbm, bf16[512,48]{1,0:T(8,128)(2,1)S(1)} %bitcast.10, bf16[2096,512]{1,0:T(8,128)(2,1)S(1)} %join.1.w_ref), custom_call_target="tpu_custom_call" | custom-call | bytes 51000000 | tf_op jit(solution)/shard_map/expert/pallas_call | solution.py:268
  83.3 8.1 %all-to-all-start.1 = ((bf16[32,520,128]{2,1,0:T(8,128)(2,1)}), bf16[32,520,128]{2,1,0:T(8,128)(2,1)}, u32[]{:S(2)}, u32[]{:S(2)}) async-start(bf16[32,520,128]{2,1,0:T(8,128)(2,1)} %get-tuple-element.27), calls=%async_computation.1 | async-start | bytes 8519680 | tf_op jit(solution)/shard_map/all_to_all | solution.py:398
  91.5 3.4 %copy-done = bf16[4,2048,512]{2,1,0:T(8,128)(2,1)S(1)} copy-done((bf16[4,2048,512]{2,1,0:T(8,128)(2,1)S(1)}, bf16[4,2048,512]{2,1,0:T(8,128)(2,1)}, u32[]{:S(2)}) %copy-start) | copy-done | bytes 8388632
  94.9 8.1 %grads.1 = (bf16[264,512]{1,0:T(8,128)(2,1)S(1)}, bf16[264,512]{1,0:T(8,128)(2,1)S(1)}, bf16[264,512]{1,0:T(8,128)(2,1)S(1)}, bf16[264,512]{1,0:T(8,128)(2,1)S(1...) custom-call(s32[1]{0:T(128)} %bitcast.4.narrow_ref, ...), custom_call_target="tpu_custom_call" | custom-call | bytes 30000000 | tf_op jit(solution)/shard_map/grads/pallas_call | solution.py:312
  103.0 1.7 %collective-permute-start.7 = (bf16[264,512]{1,0:T(8,128)(2,1)S(1)}, bf16[264,512]{1,0:T(8,128)(2,1)S(1)}, u32[]{:S(2)}, u32[]{:S(2)}) collective-permute-start(bf16[264,512]{1,0:T(8,128)(2,1)S(1)} %get-tuple-element.31), channel_id=1, source_target_pairs={{7,0},{0,1},{1,2},{2,3},{3,4},{4,5},{5,6},{6,7},{15,8},{8,9},{9,10... | collective-permute-start | bytes 811016 | tf_op jit(solution)/shard_map/ppermute | solution.py:404
  104.7 4.0 %collective-permute-start.11 = (bf16[264,512]{1,0:T(8,128)(2,1)S(1)}, bf16[264,512]{1,0:T(8,128)(2,1)S(1)}, u32[]{:S(2)}, u32[]{:S(2)}) collective-permute-start(bf16[264,512]{1,0:T(8,128)(2,1)S(1)} %get-tuple-element.35), channel_id=1, source_target_pairs={{1,0},{2,1},{3,2},{4,3},{5,4},{6,5},{7,6},{0,7},{9,8},{10,9},{11,1... | collective-permute-start | bytes 811016 | tf_op jit(solution)/shard_map/ppermute | solution.py:404
  108.8 6.5 %collective-permute-done.7 = bf16[264,512]{1,0:T(8,128)(2,1)S(1)} collective-permute-done((bf16[264,512]{1,0:T(8,128)(2,1)S(1)}, bf16[264,512]{1,0:T(8,128)(2,1)S(1)}, u32[]{:S(2)}, u32[]{:S(2)}) %collective-permute-start.7) | collective-permute-done | bytes 270368 | tf_op jit(solution)/shard_map/ppermute | solution.py:404
  115.3 0.1 add_convert_fusion.4
  115.4 0.1 collective-permute-start.8
  115.5 0.0 collective-permute-done.11
  115.5 0.1 add_convert_fusion.1
  115.5 2.7 %collective-permute-start.12 = (bf16[264,512]{1,0:T(8,128)(2,1)S(1)}, bf16[264,512]{1,0:T(8,128)(2,1)S(1)}, u32[]{:S(2)}, u32[]{:S(2)}) collective-permute-start(bf16[264,512]{1,0:T(8,128)(2,1)S(1)} %add_convert_fusion.1), channel_id=1, source_target_pairs={{1,0},{2,1},{3,2},{4,3},{5,4},{6,5},{7,6},{0,7},{9,8},{10,9},{11,1... | collective-permute-start | bytes 811016 | tf_op jit(solution)/shard_map/ppermute | solution.py:404
  118.3 5.7 %collective-permute-done.8 = bf16[264,512]{1,0:T(8,128)(2,1)S(1)} collective-permute-done((bf16[264,512]{1,0:T(8,128)(2,1)S(1)}, bf16[264,512]{1,0:T(8,128)(2,1)S(1)}, u32[]{:S(2)}, u32[]{:S(2)}) %collective-permute-start.8) | collective-permute-done | bytes 270368 | tf_op jit(solution)/shard_map/ppermute | solution.py:404
  123.9 0.1 add_convert_fusion.3
  124.0 0.1 collective-permute-start.9
  124.1 0.0 collective-permute-done.12
  124.1 0.1 add_convert_fusion
  124.2 2.7 %collective-permute-start.13 = (bf16[264,512]{1,0:T(8,128)(2,1)S(1)}, bf16[264,512]{1,0:T(8,128)(2,1)S(1)}, u32[]{:S(2)}, u32[]{:S(2)}) collective-permute-start(bf16[264,512]{1,0:T(8,128)(2,1)S(1)} %add_convert_fusion), channel_id=1, source_target_pairs={{1,0},{2,1},{3,2},{4,3},{5,4},{6,5},{7,6},{0,7},{9,8},{10,9},{11,1... | collective-permute-start | bytes 811016 | tf_op jit(solution)/shard_map/ppermute | solution.py:404
  126.9 4.8 %collective-permute-done.9 = bf16[264,512]{1,0:T(8,128)(2,1)S(1)} collective-permute-done((bf16[264,512]{1,0:T(8,128)(2,1)S(1)}, bf16[264,512]{1,0:T(8,128)(2,1)S(1)}, u32[]{:S(2)}, u32[]{:S(2)}) %collective-permute-start.9) | collective-permute-done | bytes 270368 | tf_op jit(solution)/shard_map/ppermute | solution.py:404
  131.8 0.1 add_convert_fusion.2
  131.8 0.3 collective-permute-start.10
  132.2 0.0 collective-permute-done.13.b_ref
  132.2 6.6 %collective-permute-done.10.a_ref = bf16[264,512]{1,0:T(8,128)(2,1)S(1)} collective-permute-done((bf16[264,512]{1,0:T(8,128)(2,1)S(1)}, bf16[264,512]{1,0:T(8,128)(2,1)S(1)}, u32[]{:S(2)}, u32[]{:S(2)}) %collective-permute-start.10) | collective-permute-done | bytes 270368 | tf_op jit(solution)/shard_map/ppermute | solution.py:404
  138.7 1.0 finish.1
  139.7 2.8 %all-to-all-done.1.back_hbm = bf16[32,520,128]{2,1,0:T(8,128)(2,1)} async-done(((bf16[32,520,128]{2,1,0:T(8,128)(2,1)}), bf16[32,520,128]{2,1,0:T(8,128)(2,1)}, u32[]{:S(2)}, u32[]{:S(2)}) %all-to-all-start.1) | async-done | bytes 4259872 | tf_op jit(solution)/shard_map/all_to_all | solution.py:398
  142.5 0.9 convert_reduce_fusion
  143.4 6.8 %unpack.1 = (bf16[1024,512]{1,0:T(8,128)(2,1)}, bf16[1024,512]{1,0:T(8,128)(2,1)}) custom-call(s32[1,1024]{1,0:T(1,128)S(1)} %get-tuple-element.25.pos_ref, bf16[32,520,128]{2,1,0:T(8,128)(2,1)} %all-to-all-done.1.back_hbm), custom_call_target="tpu_custom_call" | custom-call | bytes 21000000 | tf_op jit(solution)/shard_map/unpack/pallas_call | solution.py:377
  150.2 0.1 slice.19
  150.3 1.7 %collective-permute-start.14 = (f32[8,48]{1,0:T(8,128)S(1)}, f32[8,48]{1,0:T(8,128)S(1)}, u32[]{:S(2)}, u32[]{:S(2)}) collective-permute-start(f32[8,48]{1,0:T(8,128)S(1)} %slice.19), channel_id=1, source_target_pairs={{255,0},{0,1},{1,2},{2,3},{3,4},{4,5},{5,6},{6,7},{7,8},{8,9},{9,1... | collective-permute-start | bytes 4616 | tf_op jit(solution)/shard_map/ppermute | solution.py:404
  152.0 9.1 %collective-permute-done.14 = f32[8,48]{1,0:T(8,128)S(1)} collective-permute-done((f32[8,48]{1,0:T(8,128)S(1)}, f32[8,48]{1,0:T(8,128)S(1)}, u32[]{:S(2)}, u32[]{:S(2)}) %collective-permute-start.14) | collective-permute-done | bytes 1568 | tf_op jit(solution)/shard_map/ppermute | solution.py:404
  161.1 0.6 slice_add_fusion
  (16 shorter events, 0.0 us)
Async XLA Ops:
  7.5 8.8 %copy-start.11 = (bf16[1,262,512]{2,1,0:T(8,128)(2,1)S(1)}, bf16[1,262,512]{2,1,0:T(8,128)(2,1)}, u32[]{:S(2)}) copy-start(bf16[1,262,512]{2,1,0:T(8,128)(2,1)} %param.11) | copy-start | bytes 804868
  7.5 37.7 %copy-start.12 = (bf16[2048,48]{0,1:T(8,128)(2,1)S(1)}, bf16[2048,48]{0,1:T(8,128)(2,1)}, u32[]{:S(2)}) copy-start(bf16[2048,48]{0,1:T(8,128)(2,1)} %param.10) | copy-start | bytes 589828
  7.5 37.7 %slice-start = ((bf16[2048,48]{0,1:T(8,128)(2,1)}), bf16[64,48]{0,1:T(8,128)(2,1)S(1)}, s32[]{:S(2)}) async-start(bf16[2048,48]{0,1:T(8,128)(2,1)} %param.10), calls=%async_computation.2 | async-start | bytes 24576 | tf_op jit(solution)/shard_map/slice | solution.py:461
  7.5 59.7 %all-to-all-start = ((bf16[32,520,128]{2,1,0:T(8,128)(2,1)}), bf16[32,520,128]{2,1,0:T(8,128)(2,1)}, u32[]{:S(2)}, u32[]{:S(2)}) async-start(bf16[32,520,128]{2,1,0:T(8,128)(2,1)} %get-tuple-element.26), calls=%async_computation | async-start | bytes 8519680 | tf_op jit(solution)/shard_map/all_to_all | solution.py:398
  16.3 12.4 %collective-permute-start = (bf16[264,512]{1,0:T(8,128)(2,1)S(1)}, bf16[264,512]{1,0:T(8,128)(2,1)S(1)}, u32[]{:S(2)}, u32[]{:S(2)}) collective-permute-start(bf16[264,512]{1,0:T(8,128)(2,1)S(1)} %pad.4.refs_0_), channel_id=1, source_target_pairs={{7,0},{0,1},{1,2},{2,3},{3,4},{4,5},{5,6},{6,7},{15,8},{8,9},{9,10... | collective-permute-start | bytes 811016 | tf_op jit(solution)/shard_map/ppermute | solution.py:404
  18.1 10.7 %collective-permute-start.1 = (bf16[264,512]{1,0:T(8,128)(2,1)S(1)}, bf16[264,512]{1,0:T(8,128)(2,1)S(1)}, u32[]{:S(2)}, u32[]{:S(2)}) collective-permute-start(bf16[264,512]{1,0:T(8,128)(2,1)S(1)} %pad.4.refs_0_), channel_id=1, source_target_pairs={{1,0},{2,1},{3,2},{4,3},{5,4},{6,5},{7,6},{0,7},{9,8},{10,9},{11,1... | collective-permute-start | bytes 811016 | tf_op jit(solution)/shard_map/ppermute | solution.py:404
  28.7 8.6 %collective-permute-start.2 = (bf16[264,512]{1,0:T(8,128)(2,1)S(1)}, bf16[264,512]{1,0:T(8,128)(2,1)S(1)}, u32[]{:S(2)}, u32[]{:S(2)}) collective-permute-start(bf16[264,512]{1,0:T(8,128)(2,1)S(1)} %collective-permute-done.refs_1_), channel_id=1, source_target_pairs={{7,0},{0,1},{1,2},{2,3},{3,4},{4,5},{5,6},{6,7},{15,8},{8,9},{9,10... | collective-permute-start | bytes 811016 | tf_op jit(solution)/shard_map/ppermute | solution.py:404
  28.7 8.6 %collective-permute-start.3 = (bf16[264,512]{1,0:T(8,128)(2,1)S(1)}, bf16[264,512]{1,0:T(8,128)(2,1)S(1)}, u32[]{:S(2)}, u32[]{:S(2)}) collective-permute-start(bf16[264,512]{1,0:T(8,128)(2,1)S(1)} %collective-permute-done.1.refs_2_), channel_id=1, source_target_pairs={{1,0},{2,1},{3,2},{4,3},{5,4},{6,5},{7,6},{0,7},{9,8},{10,9},{11,1... | collective-permute-start | bytes 811016 | tf_op jit(solution)/shard_map/ppermute | solution.py:404
  37.4 8.4 %copy-start.1 = (bf16[264,512]{1,0:T(8,128)(2,1)}, bf16[264,512]{1,0:T(8,128)(2,1)S(1)}, u32[]{:S(2)}) copy-start(bf16[264,512]{1,0:T(8,128)(2,1)S(1)} %collective-permute-done.2.refs_3_) | copy-start | bytes 811012
  37.4 7.8 %collective-permute-start.4 = (bf16[264,512]{1,0:T(8,128)(2,1)S(1)}, bf16[264,512]{1,0:T(8,128)(2,1)S(1)}, u32[]{:S(2)}, u32[]{:S(2)}) collective-permute-start(bf16[264,512]{1,0:T(8,128)(2,1)S(1)} %collective-permute-done.2.refs_3_), channel_id=1, source_target_pairs={{7,0},{0,1},{1,2},{2,3},{3,4},{4,5},{5,6},{6,7},{15,8},{8,9},{9,10... | collective-permute-start | bytes 811016 | tf_op jit(solution)/shard_map/ppermute | solution.py:404
  37.4 14.8 %copy-start.3 = (bf16[264,512]{1,0:T(8,128)(2,1)}, bf16[264,512]{1,0:T(8,128)(2,1)S(1)}, u32[]{:S(2)}) copy-start(bf16[264,512]{1,0:T(8,128)(2,1)S(1)} %collective-permute-done.3.refs_4_) | copy-start | bytes 811012
  37.4 8.9 %collective-permute-start.5 = (bf16[264,512]{1,0:T(8,128)(2,1)S(1)}, bf16[264,512]{1,0:T(8,128)(2,1)S(1)}, u32[]{:S(2)}, u32[]{:S(2)}) collective-permute-start(bf16[264,512]{1,0:T(8,128)(2,1)S(1)} %collective-permute-done.3.refs_4_), channel_id=1, source_target_pairs={{1,0},{2,1},{3,2},{4,3},{5,4},{6,5},{7,6},{0,7},{9,8},{10,9},{11,1... | collective-permute-start | bytes 811016 | tf_op jit(solution)/shard_map/ppermute | solution.py:404
  45.2 7.0 %copy-start.5 = (bf16[264,512]{1,0:T(8,128)(2,1)}, bf16[264,512]{1,0:T(8,128)(2,1)S(1)}, u32[]{:S(2)}) copy-start(bf16[264,512]{1,0:T(8,128)(2,1)S(1)} %collective-permute-done.4.refs_5_) | copy-start | bytes 811012
  45.2 7.0 %collective-permute-start.6 = (bf16[264,512]{1,0:T(8,128)(2,1)S(1)}, bf16[264,512]{1,0:T(8,128)(2,1)S(1)}, u32[]{:S(2)}, u32[]{:S(2)}) collective-permute-start(bf16[264,512]{1,0:T(8,128)(2,1)S(1)} %collective-permute-done.4.refs_5_), channel_id=1, source_target_pairs={{7,0},{0,1},{1,2},{2,3},{3,4},{4,5},{5,6},{6,7},{15,8},{8,9},{9,10... | collective-permute-start | bytes 811016 | tf_op jit(solution)/shard_map/ppermute | solution.py:404
  46.3 0.7 copy-start.7
  52.2 0.7 copy-start.9
  52.9 1.0 copy-start.2
  53.9 1.0 copy-start.4
  54.8 1.0 copy-start.6
  55.8 1.0 copy-start.8
  56.7 1.0 copy-start.10
  83.3 59.2 %all-to-all-start.1 = ((bf16[32,520,128]{2,1,0:T(8,128)(2,1)}), bf16[32,520,128]{2,1,0:T(8,128)(2,1)}, u32[]{:S(2)}, u32[]{:S(2)}) async-start(bf16[32,520,128]{2,1,0:T(8,128)(2,1)} %get-tuple-element.27), calls=%async_computation.1 | async-start | bytes 8519680 | tf_op jit(solution)/shard_map/all_to_all | solution.py:398
  91.5 3.4 %copy-start = (bf16[4,2048,512]{2,1,0:T(8,128)(2,1)S(1)}, bf16[4,2048,512]{2,1,0:T(8,128)(2,1)}, u32[]{:S(2)}) copy-start(bf16[4,2048,512]{2,1,0:T(8,128)(2,1)} %get-tuple-element.28.z_ref) | copy-start | bytes 25165828
  103.0 12.3 %collective-permute-start.7 = (bf16[264,512]{1,0:T(8,128)(2,1)S(1)}, bf16[264,512]{1,0:T(8,128)(2,1)S(1)}, u32[]{:S(2)}, u32[]{:S(2)}) collective-permute-start(bf16[264,512]{1,0:T(8,128)(2,1)S(1)} %get-tuple-element.31), channel_id=1, source_target_pairs={{7,0},{0,1},{1,2},{2,3},{3,4},{4,5},{5,6},{6,7},{15,8},{8,9},{9,10... | collective-permute-start | bytes 811016 | tf_op jit(solution)/shard_map/ppermute | solution.py:404
  104.7 10.7 %collective-permute-start.11 = (bf16[264,512]{1,0:T(8,128)(2,1)S(1)}, bf16[264,512]{1,0:T(8,128)(2,1)S(1)}, u32[]{:S(2)}, u32[]{:S(2)}) collective-permute-start(bf16[264,512]{1,0:T(8,128)(2,1)S(1)} %get-tuple-element.35), channel_id=1, source_target_pairs={{1,0},{2,1},{3,2},{4,3},{5,4},{6,5},{7,6},{0,7},{9,8},{10,9},{11,1... | collective-permute-start | bytes 811016 | tf_op jit(solution)/shard_map/ppermute | solution.py:404
  115.4 8.6 %collective-permute-start.8 = (bf16[264,512]{1,0:T(8,128)(2,1)S(1)}, bf16[264,512]{1,0:T(8,128)(2,1)S(1)}, u32[]{:S(2)}, u32[]{:S(2)}) collective-permute-start(bf16[264,512]{1,0:T(8,128)(2,1)S(1)} %add_convert_fusion.4), channel_id=1, source_target_pairs={{7,0},{0,1},{1,2},{2,3},{3,4},{4,5},{5,6},{6,7},{15,8},{8,9},{9,10... | collective-permute-start | bytes 811016 | tf_op jit(solution)/shard_map/ppermute | solution.py:404
  115.5 8.6 %collective-permute-start.12 = (bf16[264,512]{1,0:T(8,128)(2,1)S(1)}, bf16[264,512]{1,0:T(8,128)(2,1)S(1)}, u32[]{:S(2)}, u32[]{:S(2)}) collective-permute-start(bf16[264,512]{1,0:T(8,128)(2,1)S(1)} %add_convert_fusion.1), channel_id=1, source_target_pairs={{1,0},{2,1},{3,2},{4,3},{5,4},{6,5},{7,6},{0,7},{9,8},{10,9},{11,1... | collective-permute-start | bytes 811016 | tf_op jit(solution)/shard_map/ppermute | solution.py:404
  124.0 7.8 %collective-permute-start.9 = (bf16[264,512]{1,0:T(8,128)(2,1)S(1)}, bf16[264,512]{1,0:T(8,128)(2,1)S(1)}, u32[]{:S(2)}, u32[]{:S(2)}) collective-permute-start(bf16[264,512]{1,0:T(8,128)(2,1)S(1)} %add_convert_fusion.3), channel_id=1, source_target_pairs={{7,0},{0,1},{1,2},{2,3},{3,4},{4,5},{5,6},{6,7},{15,8},{8,9},{9,10... | collective-permute-start | bytes 811016 | tf_op jit(solution)/shard_map/ppermute | solution.py:404
  124.2 8.0 %collective-permute-start.13 = (bf16[264,512]{1,0:T(8,128)(2,1)S(1)}, bf16[264,512]{1,0:T(8,128)(2,1)S(1)}, u32[]{:S(2)}, u32[]{:S(2)}) collective-permute-start(bf16[264,512]{1,0:T(8,128)(2,1)S(1)} %add_convert_fusion), channel_id=1, source_target_pairs={{1,0},{2,1},{3,2},{4,3},{5,4},{6,5},{7,6},{0,7},{9,8},{10,9},{11,1... | collective-permute-start | bytes 811016 | tf_op jit(solution)/shard_map/ppermute | solution.py:404
  131.8 6.9 %collective-permute-start.10 = (bf16[264,512]{1,0:T(8,128)(2,1)S(1)}, bf16[264,512]{1,0:T(8,128)(2,1)S(1)}, u32[]{:S(2)}, u32[]{:S(2)}) collective-permute-start(bf16[264,512]{1,0:T(8,128)(2,1)S(1)} %add_convert_fusion.2), channel_id=1, source_target_pairs={{7,0},{0,1},{1,2},{2,3},{3,4},{4,5},{5,6},{6,7},{15,8},{8,9},{9,10... | collective-permute-start | bytes 811016 | tf_op jit(solution)/shard_map/ppermute | solution.py:404
  150.3 10.8 %collective-permute-start.14 = (f32[8,48]{1,0:T(8,128)S(1)}, f32[8,48]{1,0:T(8,128)S(1)}, u32[]{:S(2)}, u32[]{:S(2)}) collective-permute-start(f32[8,48]{1,0:T(8,128)S(1)} %slice.19), channel_id=1, source_target_pairs={{255,0},{0,1},{1,2},{2,3},{3,4},{4,5},{5,6},{6,7},{7,8},{8,9},{9,1... | collective-permute-start | bytes 4616 | tf_op jit(solution)/shard_map/ppermute | solution.py:404
